TPU v7x, 256 devices: a whole 4x4x8 slice. The times are simulated.
256 devices in a mesh: snap: 8 (over z), py: 4 (over y_lo, core), pz: 8 (over y_hi, x).
Axes of the slice: x: 4, y: 4 (y_hi: 2, y_lo: 2; y = y_hi * 2 + y_lo), z: 8, core: 2. Of those that a mesh axis runs over, the one named last changes fastest.
Arguments:
- velocity: bfloat16 [8, 3, 48, 384, 1024], P('snap', None, 'pz', 'py'), may hold values from -6 to 6
- metric_x: float32 [1024], replicated, may hold values from 0.5 to 2
- metric_y: float32 [384], replicated, may hold values from 0.3 to 3
- metric_z: float32 [48], replicated, may hold values from 0.5 to 2
- sketch_matrix: float32 [8, 4], replicated, may hold values from -2 to 2
Outputs:
- sketch: float32 [4, 3, 48, 384, 1024], P(None, None, None, ('snap', 'pz'), 'py')
All inputs are finite; a program needn't handle non-finite values.
Results may differ from a plain program's by a relative error of at most 0.0065.
Values may be sent and summed in bfloat16 or wider, within the bound.
A program may use at most 128 MiB of HBM per device.

v0:
```python
import jax
import jax.numpy as jnp
from jax import lax
from jax.sharding import PartitionSpec as P

log_ratio = jnp.log((3.0 - 5.0**0.5) / 2.0)
scale_const = 5.0**0.5 / 3.0


def inverse_entry(row_index, col_index, length):
    inside = (col_index >= 0) & (col_index < length)
    column = jnp.clip(col_index, 0, length - 1)
    nearer = jnp.minimum(row_index, column).astype(jnp.float32)
    farther = jnp.maximum(row_index, column).astype(jnp.float32)
    distance = farther - nearer
    parity_sign = 1.0 - 2.0 * jnp.mod(distance, 2.0)
    magnitude = jnp.exp(distance * log_ratio) * parity_sign
    left_factor = 1.0 - jnp.exp(2.0 * (nearer + 1.0) * log_ratio)
    right_factor = 1.0 - jnp.exp(2.0 * (length - farther) * log_ratio)
    denominator = scale_const * (1.0 - jnp.exp(2.0 * (length + 1.0) * log_ratio))
    return jnp.where(inside, magnitude * left_factor * right_factor / denominator, 0.0)


def compact_table(length):
    row_index = lax.broadcasted_iota(jnp.int32, (length, length), 0)
    col_index = lax.broadcasted_iota(jnp.int32, (length, length), 1)
    first = inverse_entry(row_index, col_index - 1, length) - inverse_entry(
        row_index, col_index + 1, length
    )
    second = inverse_entry(row_index, col_index - 2, length) - inverse_entry(
        row_index, col_index + 2, length
    )
    return 7.0 / 9.0 * first + 1.0 / 36.0 * second


def split_table(length):
    table = compact_table(length)
    table_high = table.astype(jnp.bfloat16)
    table_low = (table - table_high.astype(jnp.float32)).astype(jnp.bfloat16)
    return (table_high, table_low)


def apply_split(form, tables, fields, table_first):
    table_high, table_low = tables
    if table_first:
        high_part = jnp.einsum(form, table_high, fields, preferred_element_type=jnp.float32)
        low_part = jnp.einsum(form, table_low, fields, preferred_element_type=jnp.float32)
    else:
        high_part = jnp.einsum(form, fields, table_high, preferred_element_type=jnp.float32)
        low_part = jnp.einsum(form, fields, table_low, preferred_element_type=jnp.float32)
    return high_part + low_part


def vorticity_from(zlines, metric_z):
    tables_z = split_table(zlines.shape[2])
    z_slopes = apply_split("ij,scjyx->sciyx", tables_z, zlines[:, 0:2], True)
    z_slopes = z_slopes * metric_z[None, None, :, None, None]
    slope_uz = z_slopes[:, 0]
    slope_vz = z_slopes[:, 1]
    slope_wx = zlines[:, 2].astype(jnp.float32)
    slope_wy = zlines[:, 3].astype(jnp.float32)
    spin_x = (slope_wy - slope_vz).astype(jnp.bfloat16)
    spin_y = (slope_uz - slope_wx).astype(jnp.bfloat16)
    return jnp.stack([spin_x, spin_y, zlines[:, 4]], axis=1)


def on_device(velocity, metric_x, metric_y, metric_z, sketch_matrix):
    tables_x = split_table(velocity.shape[4])
    x_slopes = apply_split("sczyj,ij->sczyi", tables_x, velocity[:, 1:3], False)
    x_slopes = (x_slopes * metric_x).astype(jnp.bfloat16)
    payload = jnp.concatenate([velocity, x_slopes], axis=1)
    ylines = lax.all_to_all(payload, "py", split_axis=4, concat_axis=3, tiled=True)
    tables_y = split_table(ylines.shape[3])
    y_slopes = apply_split("ij,sczjx->sczix", tables_y, ylines[:, 0:3:2], True)
    y_slopes = y_slopes * metric_y[None, None, None, :, None]
    slope_uy = y_slopes[:, 0]
    slope_wy = y_slopes[:, 1].astype(jnp.bfloat16)
    spin_z = (ylines[:, 3].astype(jnp.float32) - slope_uy).astype(jnp.bfloat16)
    z_payload = jnp.stack([ylines[:, 0], ylines[:, 1], ylines[:, 4], slope_wy, spin_z], axis=1)
    zlines = lax.all_to_all(
        lax.all_to_all(z_payload, "snap", split_axis=3, concat_axis=0, tiled=True),
        "pz",
        split_axis=3,
        concat_axis=2,
        tiled=True,
    )
    vorticity = vorticity_from(zlines, metric_z)
    return jnp.einsum(
        "sk,sczyx->kczyx",
        sketch_matrix,
        vorticity.astype(jnp.float32),
        precision=lax.Precision.HIGHEST,
    )


def solution(mesh):
    placed = (P("snap", None, "pz", "py", None), P(), P(), P(), P())
    return jax.shard_map(
        on_device,
        mesh=mesh,
        in_specs=placed,
        out_specs=P(None, None, None, ("snap", "pz"), "py"),
        check_vma=False,
    )
```

profile of v0, /device:TPU:30, one launch (start us, length us, event | category | flops | bytes accessed | tf_op | source)
XLA Modules:
  0.0 559.7 jit_solution(15133581711998774805)
XLA Ops:
  0.0 0.0 copy-start
  0.0 0.6 fusion.361
  0.6 0.6 fusion.367
  1.2 0.6 fusion.369
  1.8 8.1 %copy.36 = bf16[1,3,6,96,1024]{3,2,1,0,4:T(8,128)(2,1)} copy(bf16[1,3,6,96,1024]{4,3,2,1,0:T(8,128)(2,1)} %param.6) | data formatting | bytes 7077888 | tf_op args[0]
  10.0 0.0 copy-start.10
  10.0 29.3 %fusion.112 = f32[1024,2,6,96]{0,3,2,1:T(8,128)S(1)} fusion(s32[1024]{0:T(1024)S(1)} %get-tuple-element.12, s32[1024]{0:T(1024)S(1)} %get-tuple-element.13, s32[1024]{0:T(1024)S(1)} %get-tuple-element.14, s32[1024]{0:T(1024)} %get-tuple-element.15, pred[1024]{0:T(1024)(128)(4,1)} %get-tuple-element.19, pred[1024]{0:T(1024)(128)(4,1)} %get-tuple-element.18, ...), kind=kOutput, calls=%fused_computation.135 | convolution fusion | flops 2530213888 | bytes 7098368 | tf_op jit(solution)/shard_map/sczyj,ij->sczyi/dot_general | solution.py:50
  39.3 28.4 %fusion.104 = bf16[1,2,6,96,1024]{4,3,2,1,0:T(8,128)(2,1)} fusion(f32[1024,2,6,96]{0,3,2,1:T(8,128)S(1)} %fusion.112, f32[1024]{0:T(1024)S(1)} %copy-done.10, bf16[1,3,6,96,1024]{4,3,2,1,0:T(8,128)(2,1)S(1)} %copy-done.2, s32[1024]{0:T(1024)S(1)} %get-tuple-element.12, pred[1024]{0:T(1024)(128)(4,1)S(1)} %copy-done.8, s32[1024]{0:T(1024)S(1)} %get-tuple-element.13, ...), kind=kOutput, calls=%fused_computation.123 | convolution fusion | flops 2530607104 | bytes 9461760 | tf_op jit(solution)/shard_map/sczyj,ij->sczyi/dot_general | solution.py:49
  67.7 6.5 %copy.37 = bf16[1,2,6,96,1024]{3,2,1,0,4:T(8,128)(2,1)} copy(bf16[1,2,6,96,1024]{4,3,2,1,0:T(8,128)(2,1)} %fusion.104) | data formatting | bytes 4718592 | tf_op jit(solution)/shard_map/convert_element_type | solution.py:70
  74.2 10.8 %pad_maximum_fusion = bf16[1,5,6,96,1024]{3,2,1,0,4:T(8,128)(2,1)} fusion(bf16[1,2,6,96,1024]{3,2,1,0,4:T(8,128)(2,1)} %copy.37, bf16[1,3,6,96,1024]{3,2,1,0,4:T(8,128)(2,1)} %copy.36), kind=kLoop, calls=%fused_computation | loop fusion | flops 2949120 | bytes 11796480 | tf_op jit(solution)/shard_map/concatenate | solution.py:71
  85.0 6.8 %all-to-all-start = ((bf16[1,5,6,96,1024]{3,2,1,0,4:T(8,128)(2,1)}), bf16[1,5,6,96,1024]{3,2,1,0,4:T(8,128)(2,1)}, u32[]{:S(2)}, u32[]{:S(2)}) async-start(bf16[1,5,6,96,1024]{3,2,1,0,4:T(8,128)(2,1)} %pad_maximum_fusion), calls=%async_computation | async-start | bytes 20971520 | tf_op jit(solution)/shard_map/all_to_all | solution.py:72
  91.8 0.6 fusion.384
  92.4 0.6 fusion.386
  92.9 0.6 fusion.378
  93.5 112.3 %all-to-all-done = bf16[1,5,6,96,1024]{3,2,1,0,4:T(8,128)(2,1)} async-done(((bf16[1,5,6,96,1024]{3,2,1,0,4:T(8,128)(2,1)}), bf16[1,5,6,96,1024]{3,2,1,0,4:T(8,128)(2,1)}, u32[]{:S(2)}, u32[]{:S(2)}) %all-to-all-start) | async-done | bytes 5898272 | tf_op jit(solution)/shard_map/all_to_all | solution.py:72
  205.8 12.4 %copy.62 = bf16[1,5,6,96,4,256]{5,4,3,2,1,0:T(4,128)(2,1)} copy(bf16[1,5,6,96,4,256]{3,2,1,5,4,0:T(8,128)(2,1)} %bitcast.7) | data formatting | bytes 11796480 | tf_op jit(solution)/shard_map/all_to_all | solution.py:72
  218.2 3.9 copy.39
  222.0 1.7 fusion.447
  223.7 0.2 slice.55
  223.9 1.4 copy-done.1
  225.3 1.7 copy.66
  227.0 0.0 copy-start.11
  227.1 6.2 %fusion.108 = f32[2,6,256,384]{3,2,1,0:T(8,128)S(1)} fusion(bf16[1,5,6,384,256]{4,3,2,1,0:T(8,128)(2,1)} %bitcast.84, s32[384]{0:T(512)S(1)} %get-tuple-element.20, s32[384]{0:T(512)S(1)} %get-tuple-element.21, s32[384]{0:T(512)S(1)} %get-tuple-element.22, s32[384]{0:T(512)} %get-tuple-element.23, pred[384]{0:T(512)(128)(4,1)} %get-tuple-element.27, ...), kind=kOutput, calls=%fused_computation.131 | convolution fusion | flops 922042368 | bytes 7086592 | tf_op jit(solution)/shard_map/ij,sczjx->sczix/dot_general | solution.py:47
  233.3 0.0 copy-done.4
  233.3 0.0 copy-done.11
  233.3 0.0 copy-done.12
  233.4 6.4 %fusion = f32[1,2,6,384,256]{3,4,2,1,0:T(8,128)S(1)} fusion(f32[2,6,256,384]{3,2,1,0:T(8,128)S(1)} %fusion.108, f32[384]{0:T(512)S(1)} %copy-done.11, bf16[1,5,6,384,256]{4,3,2,1,0:T(8,128)(2,1)} %bitcast.85, s32[384]{0:T(512)S(1)} %get-tuple-element.20, pred[384]{0:T(512)(128)(4,1)S(1)} %copy-done.15, s32[384]{0:T(512)S(1)} %get-tuple-element.21, ...), kind=kOutput, calls=%fused_computation.15 | convolution fusion | flops 923959296 | bytes 11805696 | tf_op jit(solution)/shard_map/ij,sczjx->sczix/dot_general | solution.py:46
  239.8 1.2 slice.94
  240.9 1.4 fusion.107
  242.3 1.6 copy.43
  243.9 2.4 copy.42
  246.2 4.8 pad_maximum_fusion.1
  251.0 6.2 %copy.44 = bf16[1,5,6,384,256]{4,2,1,0,3:T(8,128)(2,1)S(1)} copy(bf16[1,5,6,384,256]{4,3,2,1,0:T(8,128)(2,1)} %pad_maximum_fusion.1) | data formatting | bytes 11796480 | tf_op jit(solution)/shard_map/stack | solution.py:79
  257.2 183.2 %all_to_all.54 = bf16[1,5,6,384,256]{4,2,1,0,3:T(8,128)(2,1)} all-to-all(bf16[1,5,6,384,256]{4,2,1,0,3:T(8,128)(2,1)S(1)} %copy.44), channel_id=1, replica_groups=mesh['snap'=8,'py'=4,'pz'=8] {'snap'}, dimensions={3} | all-to-all | bytes 11796480 | tf_op jit(solution)/shard_map/all_to_all | solution.py:81
  440.4 12.2 %copy.46 = bf16[8,5,6,48,256]{4,0,2,1,3:T(8,128)(2,1)} copy(bf16[8,5,6,48,256]{4,2,1,3,0:T(8,128)(2,1)} %bitcast.78) | data formatting | bytes 11796480 | tf_op jit(solution)/shard_map/all_to_all | solution.py:81
  452.7 7.5 %all-to-all-start.2 = ((bf16[8,5,6,48,256]{4,0,2,1,3:T(8,128)(2,1)}), bf16[8,5,6,48,256]{4,0,2,1,3:T(8,128)(2,1)}, u32[]{:S(2)}, u32[]{:S(2)}) async-start(bf16[8,5,6,48,256]{4,0,2,1,3:T(8,128)(2,1)} %copy.46), calls=%async_computation.2 | async-start | bytes 11796480 | tf_op jit(solution)/shard_map/all_to_all | solution.py:80
  460.2 81.9 %all-to-all-done.2 = bf16[8,5,6,48,256]{4,0,2,1,3:T(8,128)(2,1)} async-done(((bf16[8,5,6,48,256]{4,0,2,1,3:T(8,128)(2,1)}), bf16[8,5,6,48,256]{4,0,2,1,3:T(8,128)(2,1)}, u32[]{:S(2)}, u32[]{:S(2)}) %all-to-all-start.2) | async-done | bytes 5898272 | tf_op jit(solution)/shard_map/all_to_all | solution.py:80
  542.1 3.3 copy.48
  545.4 0.2 slice.61
  545.6 0.2 fusion.446
  545.8 0.4 copy.70
  546.3 0.0 copy-start.9
  546.3 2.1 fusion.123
  548.4 2.2 multiply_bitcast_fusion
  550.6 1.3 fusion.106
  551.9 0.4 pad_maximum_fusion.2
  552.4 4.0 fusion.130
  556.4 2.9 copy.54
  (30 shorter events, 0.1 us)
Async XLA Ops:
  0.0 552.4 %copy-start = (f32[8,4]{0,1:T(4,128)S(1)}, f32[8,4]{0,1:T(4,128)}, u32[]{:S(2)}) copy-start(f32[8,4]{0,1:T(4,128)} %param.10) | copy-start | bytes 388
  1.8 8.1 %copy-start.2 = (bf16[1,3,6,96,1024]{4,3,2,1,0:T(8,128)(2,1)S(1)}, bf16[1,3,6,96,1024]{4,3,2,1,0:T(8,128)(2,1)}, u32[]{:S(2)}) copy-start(bf16[1,3,6,96,1024]{4,3,2,1,0:T(8,128)(2,1)} %param.6) | copy-start | bytes 10616836
  9.9 29.3 %copy-start.3 = (s32[1024]{0:T(1024)S(1)}, s32[1024]{0:T(1024)}, u32[]{:S(2)}) copy-start(s32[1024]{0:T(1024)} %get-tuple-element.15) | copy-start | bytes 12292
  9.9 29.3 %copy-start.5 = (pred[1024]{0:T(1024)(128)(4,1)S(1)}, pred[1024]{0:T(1024)(128)(4,1)}, u32[]{:S(2)}) copy-start(pred[1024]{0:T(1024)(128)(4,1)} %get-tuple-element.16) | copy-start | bytes 3076
  9.9 29.4 %copy-start.6 = (pred[1024]{0:T(1024)(128)(4,1)S(1)}, pred[1024]{0:T(1024)(128)(4,1)}, u32[]{:S(2)}) copy-start(pred[1024]{0:T(1024)(128)(4,1)} %get-tuple-element.17) | copy-start | bytes 3076
  9.9 29.4 %copy-start.7 = (pred[1024]{0:T(1024)(128)(4,1)S(1)}, pred[1024]{0:T(1024)(128)(4,1)}, u32[]{:S(2)}) copy-start(pred[1024]{0:T(1024)(128)(4,1)} %get-tuple-element.18) | copy-start | bytes 3076
  9.9 29.4 %copy-start.8 = (pred[1024]{0:T(1024)(128)(4,1)S(1)}, pred[1024]{0:T(1024)(128)(4,1)}, u32[]{:S(2)}) copy-start(pred[1024]{0:T(1024)(128)(4,1)} %get-tuple-element.19) | copy-start | bytes 3076
  10.0 29.4 %copy-start.10 = (f32[1024]{0:T(1024)S(1)}, f32[1024]{0:T(1024)}, u32[]{:S(2)}) copy-start(f32[1024]{0:T(1024)} %param.7) | copy-start | bytes 12292
  85.0 120.8 %all-to-all-start = ((bf16[1,5,6,96,1024]{3,2,1,0,4:T(8,128)(2,1)}), bf16[1,5,6,96,1024]{3,2,1,0,4:T(8,128)(2,1)}, u32[]{:S(2)}, u32[]{:S(2)}) async-start(bf16[1,5,6,96,1024]{3,2,1,0,4:T(8,128)(2,1)} %pad_maximum_fusion), calls=%async_computation | async-start | bytes 20971520 | tf_op jit(solution)/shard_map/all_to_all | solution.py:72
  222.0 3.3 copy-start.1
  227.0 6.3 %copy-start.4 = (s32[384]{0:T(512)S(1)}, s32[384]{0:T(512)}, u32[]{:S(2)}) copy-start(s32[384]{0:T(512)} %get-tuple-element.23) | copy-start | bytes 4612
  227.0 6.3 %copy-start.11 = (f32[384]{0:T(512)S(1)}, f32[384]{0:T(512)}, u32[]{:S(2)}) copy-start(f32[384]{0:T(512)} %param.8) | copy-start | bytes 4612
  227.0 6.3 %copy-start.12 = (pred[384]{0:T(512)(128)(4,1)S(1)}, pred[384]{0:T(512)(128)(4,1)}, u32[]{:S(2)}) copy-start(pred[384]{0:T(512)(128)(4,1)} %get-tuple-element.24) | copy-start | bytes 1156
  227.0 6.3 %copy-start.13 = (pred[384]{0:T(512)(128)(4,1)S(1)}, pred[384]{0:T(512)(128)(4,1)}, u32[]{:S(2)}) copy-start(pred[384]{0:T(512)(128)(4,1)} %get-tuple-element.25) | copy-start | bytes 1156
  227.0 6.3 %copy-start.14 = (pred[384]{0:T(512)(128)(4,1)S(1)}, pred[384]{0:T(512)(128)(4,1)}, u32[]{:S(2)}) copy-start(pred[384]{0:T(512)(128)(4,1)} %get-tuple-element.26) | copy-start | bytes 1156
  227.0 6.3 %copy-start.15 = (pred[384]{0:T(512)(128)(4,1)S(1)}, pred[384]{0:T(512)(128)(4,1)}, u32[]{:S(2)}) copy-start(pred[384]{0:T(512)(128)(4,1)} %get-tuple-element.27) | copy-start | bytes 1156
  452.7 89.5 %all-to-all-start.2 = ((bf16[8,5,6,48,256]{4,0,2,1,3:T(8,128)(2,1)}), bf16[8,5,6,48,256]{4,0,2,1,3:T(8,128)(2,1)}, u32[]{:S(2)}, u32[]{:S(2)}) async-start(bf16[8,5,6,48,256]{4,0,2,1,3:T(8,128)(2,1)} %copy.46), calls=%async_computation.2 | async-start | bytes 11796480 | tf_op jit(solution)/shard_map/all_to_all | solution.py:80
  546.3 2.1 copy-start.9
where the time goes:
time: 571 us; the launch traced here: 560 us
  waiting for transfers between devices  194 us (34%)
  blocking collectives  183 us (32%)
  matrix products  78.6 us (14%)
  local copies, waits for them, and re-layouts  66.3 us (12%)
  other arithmetic  22.2 us (4%)
  starting transfers between devices  14.2 us (2%)
    all_to_all x1, blocking collectives, on_device(): lax.all_to_all(z_payload, 'snap', split_axis=3, concat_axis=0, tiled=True)  183 us
    all_to_all x1, waiting for transfers between devices, on_device(): lax.all_to_all(payload, 'py', split_axis=4, concat_axis=3, tiled=True)  112 us
    all_to_all x1, waiting for transfers between devices, on_device(): lax.all_to_all(lax.all_to_all(z_payload, 'snap', split_axis=3, concat_axi...  81.9 us
    dot_general x1, matrix products, apply_split(): jnp.einsum(form, fields, table_low, preferred_element_type=jnp.float32)  29.3 us
    dot_general x1, matrix products, apply_split(): jnp.einsum(form, fields, table_high, preferred_element_type=jnp.float32)  28.4 us
    all_to_all x2, local copies, waits for them, and re-layouts, on_device(): lax.all_to_all(payload, 'py', split_axis=4, concat_axis=3, tiled=True)  16.2 us
    all_to_all x1, local copies, waits for them, and re-layouts, on_device(): lax.all_to_all(z_payload, 'snap', split_axis=3, concat_axis=0, tiled=True)  12.2 us
    unnamed x35, local copies, waits for them, and re-layouts  11.7 us
  transfers between devices with their start and end apart: 2, of which 2 were waited for; matrix products, arithmetic and copies ran while one was open for 0% of the time, Pallas kernels for 0%

commit v1 on v0

v1 whole, which is shorter than its diff:
```python
import functools

import jax
import jax.numpy as jnp
import numpy as np
from jax import lax
from jax.experimental import pallas as pl
from jax.experimental.pallas import tpu as pltpu
from jax.sharding import PartitionSpec as P

MESH = pl.DeviceIdType.MESH
F32 = jnp.float32
BF16 = jnp.bfloat16
LANES = 128
NUMS = 8


def tridiagonal(n):
    return np.eye(n) + (np.eye(n, k=1) + np.eye(n, k=-1)) / 3.0


def right_side(n):
    first = np.eye(n, k=1) - np.eye(n, k=-1)
    second = np.eye(n, k=2) - np.eye(n, k=-2)
    return 7.0 / 9.0 * first + 1.0 / 36.0 * second


def derivative(n):
    return np.linalg.solve(tridiagonal(n), right_side(n))


def block_table(n):
    halo = np.zeros((n, NUMS))
    halo[0, 0], halo[0, 1], halo[1, 1] = -1.0 / 36.0, -7.0 / 9.0, -1.0 / 36.0
    halo[n - 1, 2], halo[n - 2, 2], halo[n - 1, 3] = 7.0 / 9.0, 1.0 / 36.0, 1.0 / 36.0
    halo[0, 4:6] = -1.0 / 3.0
    halo[n - 1, 6:8] = -1.0 / 3.0
    return np.linalg.solve(tridiagonal(n), np.concatenate([right_side(n), halo], axis=1))


def interface_rows(n, blocks):
    whole, size = derivative(n), n // blocks
    rows = np.zeros((blocks, NUMS, n))
    for block in range(blocks):
        low, high = block * size, (block + 1) * size
        if block > 0:
            rows[block, 0, low - 2] = 1.0
            rows[block, 1, low - 1] = 1.0
            rows[block, 4] = rows[block, 5] = whole[low - 1]
        if block < blocks - 1:
            rows[block, 2, high] = 1.0
            rows[block, 3, high + 1] = 1.0
            rows[block, 6] = rows[block, 7] = whole[high]
    return rows.reshape(blocks * NUMS, n)


def split(table):
    high = np.asarray(table, np.float32).astype(BF16)
    low = (np.asarray(table, np.float64) - high.astype(np.float64)).astype(BF16)
    return np.stack([high, low])


def dot(left, right):
    return jnp.dot(left, right, preferred_element_type=F32)


def halves(value):
    high = value.astype(BF16)
    return high, (value - high.astype(F32)).astype(BF16)


def sizes_of(mesh, shape, rank):
    snaps, nyblocks, nzblocks = mesh.shape["snap"], mesh.shape["py"], mesh.shape["pz"]
    nz, ny, nx = shape[2:]
    return dict(
        S=snaps, PY=nyblocks, PZ=nzblocks, K=rank, ZB=nz // nzblocks, YB=ny // nyblocks,
        XB=nx // nyblocks, RY=ny // snaps, RG=ny // snaps // nzblocks, NX=nx, NY=ny, NZ=nz,
    )


def tables_of(z):
    S, PY, PZ, K, RY, RG, XB, NZ = (z[n] for n in ("S", "PY", "PZ", "K", "RY", "RG", "XB", "NZ"))
    gx = np.zeros((z["NX"], LANES))
    gx[:, : PY * NUMS] = interface_rows(z["NX"], PY).T
    gy = interface_rows(z["NY"], S)
    bx, by = block_table(XB), block_table(RY)
    tx = np.zeros((2, XB + LANES, XB))
    ty = np.zeros((2, RY, RY + 16))
    for f in range(2):
        tx[f, :XB] = bx[:, :XB].T
        tx[f, XB + NUMS * f : XB + NUMS * (f + 1)] = bx[:, XB:].T
        ty[f, :, :RY] = by[:, :RY]
        ty[f, :, RY + NUMS * f : RY + NUMS * (f + 1)] = by[:, RY:]
    dz = np.einsum("zw,ij->izwj", derivative(NZ), np.eye(8)).reshape(8 * NZ, 8 * NZ)
    turn = np.einsum("zw,ij->izwj", np.eye(NZ), np.eye(8)).reshape(8 * NZ, 8 * NZ)
    rows = 2 * K * RY
    gather = np.zeros((rows, rows))
    groups = K * RG // 8
    for zz in range(2):
        for k in range(K):
            for q in range(PZ):
                for r in range(RG):
                    g, i = divmod(k * RG + r, 8)
                    gather[((q * groups + g) * 2 + zz) * 8 + i, (zz * K + k) * RY + q * RG + r] = 1.0
    one = lambda t: jnp.asarray(t.astype(np.float32)).astype(BF16)
    return [jnp.asarray(split(t)) for t in (gx, gy, tx, ty, dz)] + [one(turn), one(gather)]


def body(
    z, vel, gx, gy, tx, ty, dz, turn, gather, mx, my, mz, sk, out,
    vw, ef, es, buf_a, buf_e, buf_y, buf_c, buf_cy, buf_ce, se, xh, xl, yh, yl, pb, buf_bs, buf_r,
    send_a, recv_a, send_e, recv_e, send_c, recv_c, send_cy, recv_cy, send_ce, recv_ce, send_b, recv_b,
    local_v, local_a, local_e, local_c, local_cy, local_ce, local_b,
):
    S, PY, PZ, K, ZB, YB, XB, RY, RG = (z[n] for n in ("S", "PY", "PZ", "K", "ZB", "YB", "XB", "RY", "RG"))
    groups, fields = K * RG // 8, 7
    me_s, me_y, me_z = lax.axis_index("snap"), lax.axis_index("py"), lax.axis_index("pz")

    def other(me, d, n):
        return lax.rem(me + d, n)

    def remote(src, dst, send, recv, axis, peer):
        return pltpu.make_async_remote_copy(
            src_ref=src, dst_ref=dst, send_sem=send, recv_sem=recv, device_id={axis: peer}, device_id_type=MESH)

    def mult(value, size):
        return pl.ds(pl.multiple_of(value * size, size), size)

    def a_copy(p, d):
        peer = other(me_y, d, PY)
        return remote(vel.at[0, :, p, :, mult(peer, XB)], buf_a.at[p, :, mult(me_y, YB), :],
                      send_a.at[p, d - 1], recv_a.at[p, d - 1], "py", peer)

    def a_local(p):
        return pltpu.make_async_copy(vel.at[0, :, p, :, mult(me_y, XB)], buf_a.at[p, :, mult(me_y, YB), :], local_a.at[p])

    def e_copy(d):
        peer = other(me_y, d, PY)
        return remote(es.at[peer], buf_e.at[mult(me_y, YB), :], send_e.at[d - 1], recv_e.at[d - 1], "py", peer)

    def e_local():
        return pltpu.make_async_copy(es.at[me_y], buf_e.at[mult(me_y, YB), :], local_e.at[0])

    def c_copy(p, d):
        peer = other(me_s, d, S)
        return remote(buf_a.at[p, :, mult(peer, RY), :], buf_c.at[me_s, p],
                      send_c.at[p, d - 1], recv_c.at[p, d - 1], "snap", peer)

    def c_local(p):
        return pltpu.make_async_copy(buf_a.at[p, :, mult(me_s, RY), :], buf_c.at[me_s, p], local_c.at[p])

    def cy_copy(p, d):
        peer = other(me_s, d, S)
        return remote(buf_y.at[p, peer], buf_cy.at[me_s, p],
                      send_cy.at[p, d - 1], recv_cy.at[p, d - 1], "snap", peer)

    def cy_local(p):
        return pltpu.make_async_copy(buf_y.at[p, me_s], buf_cy.at[me_s, p], local_cy.at[p])

    def ce_copy(d):
        peer = other(me_s, d, S)
        return remote(buf_e.at[mult(peer, RY), :], buf_ce.at[me_s], send_ce.at[d - 1], recv_ce.at[d - 1], "snap", peer)

    def ce_local():
        return pltpu.make_async_copy(buf_e.at[mult(me_s, RY), :], buf_ce.at[me_s], local_ce.at[0])

    def b_rows(pp):
        return pl.ds(pl.multiple_of((me_z * (ZB // 2) + pp) * 16, 16), 16)

    def b_copy(pp, d):
        peer = other(me_z, d, PZ)
        return remote(buf_bs.at[pp, peer], buf_r.at[:, b_rows(pp), :],
                      send_b.at[pp, d - 1], recv_b.at[pp, d - 1], "pz", peer)

    def b_local(pp):
        return pltpu.make_async_copy(buf_bs.at[pp, me_z], buf_r.at[:, b_rows(pp), :], local_b.at[pp])

    planes_in = pltpu.make_async_copy(vel.at[0, 1:3], vw, local_v.at[0])
    planes_in.start()
    for p in range(ZB):
        a_local(p).start()

    barrier = pltpu.get_barrier_semaphore()
    for axis, me, n in (("py", me_y, PY), ("snap", me_s, S), ("pz", me_z, PZ)):
        for d in range(1, n):
            pl.semaphore_signal(barrier, inc=1, device_id={axis: other(me, d, n)}, device_id_type=MESH)
    pl.semaphore_wait(barrier, PY + S + PZ - 3)

    for p in range(ZB):
        for d in range(1, PY):
            a_copy(p, d).start()

    planes_in.wait()
    lane = lax.broadcasted_iota(jnp.int32, (YB, LANES), 1)
    for f in range(2):
        for p in range(ZB):
            j = 2 * p + f
            line = vw[f, p]
            ef[j] = dot(line, gx[0]) + dot(line, gx[1])
    for b in range(PY):
        total = jnp.zeros((YB, LANES), F32)
        for j in range(2 * ZB):
            shifted = pltpu.roll(ef[j], (NUMS * (j - b)) % LANES, 1)
            total = jnp.where((lane >= NUMS * j) & (lane < NUMS * (j + 1)), shifted, total)
        rounded = total.astype(BF16).astype(F32)
        low = (lane % NUMS == 5) | (lane % NUMS == 7)
        es[b] = jnp.where(low, total - rounded, rounded).astype(BF16)
    for d in range(1, PY):
        e_copy(d).start()
    e_local().start()

    def a_stage(p):
        a_local(p).wait()
        for d in range(1, PY):
            a_copy(p, d).wait_recv()
        row = lax.broadcasted_iota(jnp.int32, (S * NUMS, XB), 0)
        low = (row % NUMS == 5) | (row % NUMS == 7)
        parts = []
        for f in (0, 2):
            field = buf_a[p, f]
            numbers = dot(gy[0], field) + dot(gy[1], field)
            rounded = numbers.astype(BF16).astype(F32)
            parts.append(jnp.where(low, numbers - rounded, rounded))
        for s in range(S):
            cut = slice(NUMS * s, NUMS * (s + 1))
            buf_y[p, s] = jnp.concatenate([parts[0][cut], parts[1][cut]], axis=0).astype(BF16)
        for d in range(1, S):
            c_copy(p, d).start()
            cy_copy(p, d).start()
        c_local(p).start()
        cy_local(p).start()

    def e_stage():
        e_local().wait()
        for d in range(1, PY):
            e_copy(d).wait_recv()
        for d in range(1, S):
            ce_copy(d).start()
        ce_local().start()

    def se_stage():
        ce_local().wait()
        for d in range(1, S):
            ce_copy(d).wait_recv()
        for k in range(K):
            total = sk[0, k] * buf_ce[0].astype(F32)
            for s in range(1, S):
                total = total + sk[s, k] * buf_ce[s].astype(F32)
            se[RY * k : RY * (k + 1), :] = total

    def s_stage(p):
        c_local(p).wait()
        cy_local(p).wait()
        for d in range(1, S):
            c_copy(p, d).wait_recv()
            cy_copy(p, d).wait_recv()
        base = lax.rem(p, 2) * (K * RY)

        def sketch(parts, k):
            total = sk[0, k] * parts[0]
            for s in range(1, S):
                total = total + sk[s, k] * parts[s]
            return halves(total)

        for f in range(3):
            for t in range(RY // 16):
                rows = slice(16 * t, 16 * (t + 1))
                parts = [buf_c[s, p, f, rows, :].astype(F32) for s in range(S)]
                for k in range(K):
                    high, low = sketch(parts, k)
                    if f != 1:
                        yh[f // 2, rows, XB * k : XB * (k + 1)] = high
                        yl[f // 2, rows, XB * k : XB * (k + 1)] = low
                    own = slice(RY * k + 16 * t, RY * k + 16 * (t + 1))
                    if f != 0:
                        xh[f - 1, own, :XB] = high
                        xl[f - 1, own, :XB] = low
                    if f != 2:
                        dest = pl.ds(pl.multiple_of(base + RY * k + 16 * t, 16), 16)
                        pb[2 * f, dest, :] = high
                        pb[2 * f + 1, dest, :] = low
        parts = [buf_cy[s, p].astype(F32) for s in range(S)]
        for k in range(K):
            high, low = sketch(parts, k)
            for f in range(2):
                yh[f, RY : RY + 16, XB * k : XB * (k + 1)] = high
                yl[f, RY : RY + 16, XB * k : XB * (k + 1)] = low
        high, low = halves(pltpu.roll(se[...], lax.rem(LANES - 2 * NUMS * p, LANES), 1))
        for f in range(2):
            xh[f, :, XB:] = high
            xl[f, :, XB:] = low

        x_slopes = [dot(xh[f], tx[0, f]) + dot(xl[f], tx[0, f]) + dot(xh[f], tx[1, f]) for f in range(2)]
        y_slopes = [dot(ty[0, f], yh[f]) + dot(ty[0, f], yl[f]) + dot(ty[1, f], yh[f]) for f in range(2)]
        scale_x = mx[0:1, mult(me_y, XB)]
        scale_y = jnp.tile(my[mult(me_s, RY), :], (1, XB // LANES))
        for k in range(K):
            own, cols = slice(RY * k, RY * (k + 1)), slice(XB * k, XB * (k + 1))
            dest = pl.ds(pl.multiple_of(base + RY * k, 16), RY)
            pb[4, dest, :] = (x_slopes[1][own] * scale_x).astype(BF16)
            pb[5, dest, :] = (y_slopes[1][:, cols] * scale_y).astype(BF16)
            pb[6, dest, :] = (x_slopes[0][own] * scale_x - y_slopes[0][:, cols] * scale_y).astype(BF16)

        @pl.when(lax.rem(p, 2) == 1)
        def _():
            pp = p // 2
            for f in range(fields):
                moved = dot(gather[...], pb[f]).astype(BF16)
                for q in range(PZ):
                    for g in range(groups):
                        cut = (q * groups + g) * 16
                        buf_bs[pp, q, g * fields + f] = moved[cut : cut + 16]
            for d in range(1, PZ):
                b_copy(pp, d).start()
            b_local(pp).start()

    lag = min(3, ZB)

    @pl.loop(0, ZB + lag)
    def _(i):
        @pl.when(i < ZB)
        def _():
            a_stage(i)

        @pl.when(i == 1)
        def _():
            e_stage()

        @pl.when(i == lag)
        def _():
            se_stage()

        @pl.when(i >= lag)
        def _():
            s_stage(i - lag)

    for pp in range(ZB // 2):
        b_local(pp).wait()
        for d in range(1, PZ):
            b_copy(pp, d).wait_recv()
    NZ = z["NZ"]
    scale_z = jnp.tile(mz[...], (1, XB // LANES))
    for g in range(groups):
        at = g * fields
        slope = [
            dot(dz[0], buf_r[at + 2 * f]) + dot(dz[0], buf_r[at + 2 * f + 1]) + dot(dz[1], buf_r[at + 2 * f]) for f in range(2)
        ]
        w_x, w_y, spin_z = (dot(turn[...], buf_r[at + f]) for f in (4, 5, 6))
        for i in range(8):
            k, r = divmod(8 * g + i, RG)
            cut = slice(NZ * i, NZ * (i + 1))
            out[k, 0, r] = w_y[cut] - slope[1][cut] * scale_z
            out[k, 1, r] = slope[0][cut] * scale_z - w_x[cut]
            out[k, 2, r] = spin_z[cut]

    for p in range(ZB):
        for d in range(1, PY):
            a_copy(p, d).wait_send()
        for d in range(1, S):
            c_copy(p, d).wait_send()
            cy_copy(p, d).wait_send()
    for d in range(1, PY):
        e_copy(d).wait_send()
    for d in range(1, S):
        ce_copy(d).wait_send()
    for pp in range(ZB // 2):
        for d in range(1, PZ):
            b_copy(pp, d).wait_send()


def solution(mesh):
    def step(velocity, metric_x, metric_y, metric_z, sketch_matrix):
        whole = (1, 3, velocity.shape[2] * mesh.shape["pz"], velocity.shape[3] * mesh.shape["py"], velocity.shape[4])
        z = sizes_of(mesh, whole, sketch_matrix.shape[1])
        S, PY, PZ, K, ZB, YB, XB, RY, RG, NX, NY, NZ = (z[n] for n in (
            "S", "PY", "PZ", "K", "ZB", "YB", "XB", "RY", "RG", "NX", "NY", "NZ"))
        tables = tables_of(z)
        my = jnp.broadcast_to(metric_y[:, None], (NY, LANES))
        mz = jnp.broadcast_to(metric_z[:, None], (NZ, LANES))
        groups, fields = K * RG // 8, 7
        dma = pltpu.SemaphoreType.DMA
        vmem = pl.BlockSpec(memory_space=pltpu.VMEM)
        result = pl.pallas_call(
            functools.partial(body, z),
            out_shape=jax.ShapeDtypeStruct((K, 3, RG, NZ, XB), F32),
            in_specs=[pl.BlockSpec(memory_space=pl.ANY)] + [vmem] * 10 + [pl.BlockSpec(memory_space=pltpu.SMEM)],
            out_specs=vmem,
            scratch_shapes=[
                pltpu.VMEM((2, ZB, YB, NX), BF16),
                pltpu.VMEM((2 * ZB, YB, LANES), F32),
                pltpu.VMEM((PY, YB, LANES), BF16),
                pltpu.VMEM((ZB, 3, NY, XB), BF16),
                pltpu.VMEM((NY, LANES), BF16),
                pltpu.VMEM((ZB, S, 16, XB), BF16),
                pltpu.VMEM((S, ZB, 3, RY, XB), BF16),
                pltpu.VMEM((S, ZB, 16, XB), BF16),
                pltpu.VMEM((S, RY, LANES), BF16),
                pltpu.VMEM((K * RY, LANES), F32),
                pltpu.VMEM((2, K * RY, XB + LANES), BF16),
                pltpu.VMEM((2, K * RY, XB + LANES), BF16),
                pltpu.VMEM((2, RY + 16, K * XB), BF16),
                pltpu.VMEM((2, RY + 16, K * XB), BF16),
                pltpu.VMEM((fields, 2 * K * RY, XB), BF16),
                pltpu.VMEM((ZB // 2, PZ, groups * fields, 16, XB), BF16),
                pltpu.VMEM((groups * fields, 8 * NZ, XB), BF16),
                dma((ZB, PY - 1)), dma((ZB, PY - 1)), dma((PY - 1,)), dma((PY - 1,)),
                dma((ZB, S - 1)), dma((ZB, S - 1)), dma((ZB, S - 1)), dma((ZB, S - 1)),
                dma((S - 1,)), dma((S - 1,)), dma((ZB // 2, PZ - 1)), dma((ZB // 2, PZ - 1)),
                dma((1,)), dma((ZB,)), dma((1,)), dma((ZB,)), dma((ZB,)), dma((1,)), dma((ZB // 2,)),
            ],
            compiler_params=pltpu.CompilerParams(
                collective_id=0, has_side_effects=True, vmem_limit_bytes=60 * 1024 * 1024),
        )(velocity, *tables, metric_x[None, :], my, mz, sketch_matrix)
        return jnp.swapaxes(result, 2, 3)

    return jax.shard_map(
        step,
        mesh=mesh,
        in_specs=(P("snap", None, "pz", "py", None), P(), P(), P(), P()),
        out_specs=P(None, None, None, ("snap", "pz"), "py"),
        check_vma=False,
    )
```

time: 571 us -> 149 us (0.26)
  the two profiles are of different devices: /device:TPU:30 before, /device:TPU:1 now
where the time goes in v1:
time: 149 us; the launch traced here: 147 us
  Pallas kernels  139 us (93%)
  local copies, waits for them, and re-layouts  8.2 us (6%)
    pallas_call x1, Pallas kernels, step(): pl.pallas_call(functools.partial(body, z), out_shape=jax.ShapeDtypeStruct...  139 us
    unnamed x2, local copies, waits for them, and re-layouts  5.41 us

profile of v1, /device:TPU:1, one launch (start us, length us, event | category | flops | bytes accessed | tf_op | source)
XLA Modules:
  0.0 147.0 jit_solution(16211723234787650194)
XLA Ops:
  0.0 1.3 copy.13.sk
  1.3 1.3 broadcast_in_dim.8.mz
  2.7 1.5 %broadcast_in_dim.7.my = f32[384,128]{1,0:T(8,128)} broadcast(f32[384]{0:T(512)} %param.14), dimensions={0} | broadcast | bytes 198144 | tf_op jit(solution)/shard_map/broadcast_in_dim | solution.py:378
  4.1 138.8 %shard_map.118 = f32[4,3,6,48,256]{4,3,2,1,0:T(8,128)} custom-call(bf16[1,3,6,96,1024]{4,3,2,1,0:T(8,128)(2,1)} %vel.1, bf16[2,1024,128]{2,1,0:T(8,128)(2,1)} %constant.14.clone.gx, bf16[2,64,384]{2,1,0:T(8,128)(2,1)} %constant.15.clone.gy, bf16[2,2,384,256]{3,2,1,0:T(8,128)(2,1)} %constant.16.clone.tx, bf16[2,2,48,64]{3,2,1,0:T(8,128)(2,1)} %constant.17.clone.ty, ...), custom_call_target="tpu_custom_call" | custom-call | tf_op jit(solution)/shard_map/pallas_call | solution.py:383
  142.9 4.1 %copy.15 = f32[4,3,48,6,256]{4,2,3,1,0:T(8,128)} copy(f32[4,3,48,6,256]{4,2,3,1,0:T(8,128)} %bitcast.2) | data formatting | bytes 7077888

commit v2 on v1

--- a/solution.py
+++ b/solution.py
@@ -93,24 +93,23 @@
         ty[f, :, RY + NUMS * f : RY + NUMS * (f + 1)] = by[:, RY:]
     dz = np.einsum("zw,ij->izwj", derivative(NZ), np.eye(8)).reshape(8 * NZ, 8 * NZ)
     turn = np.einsum("zw,ij->izwj", np.eye(NZ), np.eye(8)).reshape(8 * NZ, 8 * NZ)
-    rows = 2 * K * RY
-    gather = np.zeros((rows, rows))
+    gather = np.zeros((K * RY, K * RY))
     groups = K * RG // 8
-    for zz in range(2):
-        for k in range(K):
-            for q in range(PZ):
-                for r in range(RG):
-                    g, i = divmod(k * RG + r, 8)
-                    gather[((q * groups + g) * 2 + zz) * 8 + i, (zz * K + k) * RY + q * RG + r] = 1.0
+    for k in range(K):
+        for q in range(PZ):
+            for r in range(RG):
+                g, i = divmod(r * K + k, 8)
+                gather[(q * groups + g) * 8 + i, k * RY + q * RG + r] = 1.0
     one = lambda t: jnp.asarray(t.astype(np.float32)).astype(BF16)
-    return [jnp.asarray(split(t)) for t in (gx, gy, tx, ty, dz)] + [one(turn), one(gather)]
+    return [jnp.asarray(split(t)) for t in (gx, gy, tx, ty)] + [one(gather)], [jnp.asarray(split(dz)), one(turn)]
 
 
 def body(
-    z, vel, gx, gy, tx, ty, dz, turn, gather, mx, my, mz, sk, out,
-    vw, ef, es, buf_a, buf_e, buf_y, buf_c, buf_cy, buf_ce, se, xh, xl, yh, yl, pb, buf_bs, buf_r,
+    z, vel, gx_in, gy_in, tx_in, ty_in, gather_in, mx, my, sk, out,
+    gx, gy, tx, ty, gather, scale_y,
+    vw, ef, es, buf_a, buf_e, buf_y, buf_c, buf_cy, buf_ce, se, xh, xl, yh, yl, pb, buf_bs,
     send_a, recv_a, send_e, recv_e, send_c, recv_c, send_cy, recv_cy, send_ce, recv_ce, send_b, recv_b,
-    local_v, local_a, local_e, local_c, local_cy, local_ce, local_b,
+    local_t, local_v, local_a, local_e, local_c, local_cy, local_ce, local_b,
 ):
     S, PY, PZ, K, ZB, YB, XB, RY, RG = (z[n] for n in ("S", "PY", "PZ", "K", "ZB", "YB", "XB", "RY", "RG"))
     groups, fields = K * RG // 8, 7
@@ -126,10 +125,10 @@
     def mult(value, size):
         return pl.ds(pl.multiple_of(value * size, size), size)
 
-    def a_copy(p, d):
+    def a_copy(p, f, d):
         peer = other(me_y, d, PY)
-        return remote(vel.at[0, :, p, :, mult(peer, XB)], buf_a.at[p, :, mult(me_y, YB), :],
-                      send_a.at[p, d - 1], recv_a.at[p, d - 1], "py", peer)
+        return remote(vel.at[0, f, p, :, mult(peer, XB)], buf_a.at[p, f, mult(me_y, YB), :],
+                      send_a.at[p, f, d - 1], recv_a.at[p, f, d - 1], "py", peer)
 
     def a_local(p):
         return pltpu.make_async_copy(vel.at[0, :, p, :, mult(me_y, XB)], buf_a.at[p, :, mult(me_y, YB), :], local_a.at[p])
@@ -141,10 +140,10 @@
     def e_local():
         return pltpu.make_async_copy(es.at[me_y], buf_e.at[mult(me_y, YB), :], local_e.at[0])
 
-    def c_copy(p, d):
+    def c_copy(p, f, d):
         peer = other(me_s, d, S)
-        return remote(buf_a.at[p, :, mult(peer, RY), :], buf_c.at[me_s, p],
-                      send_c.at[p, d - 1], recv_c.at[p, d - 1], "snap", peer)
+        return remote(buf_a.at[p, f, mult(peer, RY), :], buf_c.at[me_s, p, f],
+                      send_c.at[p, f, d - 1], recv_c.at[p, f, d - 1], "snap", peer)
 
     def c_local(p):
         return pltpu.make_async_copy(buf_a.at[p, :, mult(me_s, RY), :], buf_c.at[me_s, p], local_c.at[p])
@@ -164,21 +163,16 @@
     def ce_local():
         return pltpu.make_async_copy(buf_e.at[mult(me_s, RY), :], buf_ce.at[me_s], local_ce.at[0])
 
-    def b_rows(pp):
-        return pl.ds(pl.multiple_of((me_z * (ZB // 2) + pp) * 16, 16), 16)
-
-    def b_copy(pp, d):
+    def b_rows(p):
+        return pl.ds(pl.multiple_of((me_z * ZB + p) * 8, 8), 8)
+
+    def b_copy(p, d):
         peer = other(me_z, d, PZ)
-        return remote(buf_bs.at[pp, peer], buf_r.at[:, b_rows(pp), :],
-                      send_b.at[pp, d - 1], recv_b.at[pp, d - 1], "pz", peer)
-
-    def b_local(pp):
-        return pltpu.make_async_copy(buf_bs.at[pp, me_z], buf_r.at[:, b_rows(pp), :], local_b.at[pp])
-
-    planes_in = pltpu.make_async_copy(vel.at[0, 1:3], vw, local_v.at[0])
-    planes_in.start()
-    for p in range(ZB):
-        a_local(p).start()
+        return remote(buf_bs.at[p, peer], out.at[:, b_rows(p), :],
+                      send_b.at[p, d - 1], recv_b.at[p, d - 1], "pz", peer)
+
+    def b_local(p):
+        return pltpu.make_async_copy(buf_bs.at[p, me_z], out.at[:, b_rows(p), :], local_b.at[p])
 
     barrier = pltpu.get_barrier_semaphore()
     for axis, me, n in (("py", me_y, PY), ("snap", me_s, S), ("pz", me_z, PZ)):
@@ -187,10 +181,23 @@
     pl.semaphore_wait(barrier, PY + S + PZ - 3)
 
     for p in range(ZB):
-        for d in range(1, PY):
-            a_copy(p, d).start()
+        for f in range(3):
+            for d in range(1, PY):
+                a_copy(p, f, d).start()
+        a_local(p).start()
+    planes_in = pltpu.make_async_copy(vel.at[0, 1:3], vw, local_v.at[0])
+    planes_in.start()
+    tables = [
+        pltpu.make_async_copy(src, dst, local_t.at[t])
+        for t, (src, dst) in enumerate(((gx_in, gx), (gy_in, gy), (tx_in, tx), (ty_in, ty), (gather_in, gather)))
+    ]
+    for table in tables:
+        table.start()
+    for r in range(RY):
+        scale_y[r : r + 1, :] = jnp.full((1, XB), my[me_s * RY + r], F32)
 
     planes_in.wait()
+    tables[0].wait()
     lane = lax.broadcasted_iota(jnp.int32, (YB, LANES), 1)
     for f in range(2):
         for p in range(ZB):
@@ -209,10 +216,16 @@
         e_copy(d).start()
     e_local().start()
 
+    tables[1].wait()
+
     def a_stage(p):
         a_local(p).wait()
-        for d in range(1, PY):
-            a_copy(p, d).wait_recv()
+        for f in range(3):
+            for d in range(1, PY):
+                a_copy(p, f, d).wait_recv()
+            for d in range(1, S):
+                c_copy(p, f, d).start()
+        c_local(p).start()
         row = lax.broadcasted_iota(jnp.int32, (S * NUMS, XB), 0)
         low = (row % NUMS == 5) | (row % NUMS == 7)
         parts = []
@@ -225,9 +238,7 @@
             cut = slice(NUMS * s, NUMS * (s + 1))
             buf_y[p, s] = jnp.concatenate([parts[0][cut], parts[1][cut]], axis=0).astype(BF16)
         for d in range(1, S):
-            c_copy(p, d).start()
             cy_copy(p, d).start()
-        c_local(p).start()
         cy_local(p).start()
 
     def e_stage():
@@ -239,27 +250,29 @@
         ce_local().start()
 
     def se_stage():
+        for table in tables[2:]:
+            table.wait()
         ce_local().wait()
         for d in range(1, S):
             ce_copy(d).wait_recv()
         for k in range(K):
-            total = sk[0, k] * buf_ce[0].astype(F32)
+            total = sk[k, 0] * buf_ce[0].astype(F32)
             for s in range(1, S):
-                total = total + sk[s, k] * buf_ce[s].astype(F32)
+                total = total + sk[k, s] * buf_ce[s].astype(F32)
             se[RY * k : RY * (k + 1), :] = total
 
     def s_stage(p):
         c_local(p).wait()
         cy_local(p).wait()
         for d in range(1, S):
-            c_copy(p, d).wait_recv()
+            for f in range(3):
+                c_copy(p, f, d).wait_recv()
             cy_copy(p, d).wait_recv()
-        base = lax.rem(p, 2) * (K * RY)
 
         def sketch(parts, k):
-            total = sk[0, k] * parts[0]
+            total = sk[k, 0] * parts[0]
             for s in range(1, S):
-                total = total + sk[s, k] * parts[s]
+                total = total + sk[k, s] * parts[s]
             return halves(total)
 
         for f in range(3):
@@ -276,9 +289,8 @@
                         xh[f - 1, own, :XB] = high
                         xl[f - 1, own, :XB] = low
                     if f != 2:
-                        dest = pl.ds(pl.multiple_of(base + RY * k + 16 * t, 16), 16)
-                        pb[2 * f, dest, :] = high
-                        pb[2 * f + 1, dest, :] = low
+                        pb[2 * f, own, :] = high
+                        pb[2 * f + 1, own, :] = low
         parts = [buf_cy[s, p].astype(F32) for s in range(S)]
         for k in range(K):
             high, low = sketch(parts, k)
@@ -293,26 +305,20 @@
         x_slopes = [dot(xh[f], tx[0, f]) + dot(xl[f], tx[0, f]) + dot(xh[f], tx[1, f]) for f in range(2)]
         y_slopes = [dot(ty[0, f], yh[f]) + dot(ty[0, f], yl[f]) + dot(ty[1, f], yh[f]) for f in range(2)]
         scale_x = mx[0:1, mult(me_y, XB)]
-        scale_y = jnp.tile(my[mult(me_s, RY), :], (1, XB // LANES))
         for k in range(K):
             own, cols = slice(RY * k, RY * (k + 1)), slice(XB * k, XB * (k + 1))
-            dest = pl.ds(pl.multiple_of(base + RY * k, 16), RY)
-            pb[4, dest, :] = (x_slopes[1][own] * scale_x).astype(BF16)
-            pb[5, dest, :] = (y_slopes[1][:, cols] * scale_y).astype(BF16)
-            pb[6, dest, :] = (x_slopes[0][own] * scale_x - y_slopes[0][:, cols] * scale_y).astype(BF16)
-
-        @pl.when(lax.rem(p, 2) == 1)
-        def _():
-            pp = p // 2
-            for f in range(fields):
-                moved = dot(gather[...], pb[f]).astype(BF16)
-                for q in range(PZ):
-                    for g in range(groups):
-                        cut = (q * groups + g) * 16
-                        buf_bs[pp, q, g * fields + f] = moved[cut : cut + 16]
-            for d in range(1, PZ):
-                b_copy(pp, d).start()
-            b_local(pp).start()
+            pb[4, own, :] = (x_slopes[1][own] * scale_x).astype(BF16)
+            pb[5, own, :] = (y_slopes[1][:, cols] * scale_y[...]).astype(BF16)
+            pb[6, own, :] = (x_slopes[0][own] * scale_x - y_slopes[0][:, cols] * scale_y[...]).astype(BF16)
+        for f in range(fields):
+            moved = dot(gather[...], pb[f]).astype(BF16)
+            for q in range(PZ):
+                for g in range(groups):
+                    cut = (q * groups + g) * 8
+                    buf_bs[p, q, g * fields + f] = moved[cut : cut + 8]
+        for d in range(1, PZ):
+            b_copy(p, d).start()
+        b_local(p).start()
 
     lag = min(3, ZB)
 
@@ -334,38 +340,39 @@
         def _():
             s_stage(i - lag)
 
-    for pp in range(ZB // 2):
-        b_local(pp).wait()
+    for p in range(ZB):
+        b_local(p).wait()
         for d in range(1, PZ):
-            b_copy(pp, d).wait_recv()
-    NZ = z["NZ"]
-    scale_z = jnp.tile(mz[...], (1, XB // LANES))
-    for g in range(groups):
-        at = g * fields
-        slope = [
-            dot(dz[0], buf_r[at + 2 * f]) + dot(dz[0], buf_r[at + 2 * f + 1]) + dot(dz[1], buf_r[at + 2 * f]) for f in range(2)
-        ]
-        w_x, w_y, spin_z = (dot(turn[...], buf_r[at + f]) for f in (4, 5, 6))
-        for i in range(8):
-            k, r = divmod(8 * g + i, RG)
-            cut = slice(NZ * i, NZ * (i + 1))
-            out[k, 0, r] = w_y[cut] - slope[1][cut] * scale_z
-            out[k, 1, r] = slope[0][cut] * scale_z - w_x[cut]
-            out[k, 2, r] = spin_z[cut]
+            b_copy(p, d).wait_recv()
 
     for p in range(ZB):
-        for d in range(1, PY):
-            a_copy(p, d).wait_send()
+        for f in range(3):
+            for d in range(1, PY):
+                a_copy(p, f, d).wait_send()
+            for d in range(1, S):
+                c_copy(p, f, d).wait_send()
         for d in range(1, S):
-            c_copy(p, d).wait_send()
             cy_copy(p, d).wait_send()
+        for d in range(1, PZ):
+            b_copy(p, d).wait_send()
     for d in range(1, PY):
         e_copy(d).wait_send()
     for d in range(1, S):
         ce_copy(d).wait_send()
-    for pp in range(ZB // 2):
-        for d in range(1, PZ):
-            b_copy(pp, d).wait_send()
+
+
+def z_body(z, lines, dz, turn, mz, out):
+    K, NZ, XB = z["K"], z["NZ"], z["XB"]
+    same = lax.broadcasted_iota(jnp.int32, (NZ, NZ), 0) == lax.broadcasted_iota(jnp.int32, (NZ, NZ), 1)
+    scale_z = jnp.broadcast_to(jnp.sum(jnp.where(same, mz[...], 0.0), axis=1, keepdims=True), (NZ, XB))
+    slope = [dot(dz[0], lines[2 * f]) + dot(dz[0], lines[2 * f + 1]) + dot(dz[1], lines[2 * f]) for f in range(2)]
+    w_x, w_y, spin_z = (dot(turn[...], lines[f]) for f in (4, 5, 6))
+    for i in range(8):
+        r, k = divmod(i, K)
+        cut = slice(NZ * i, NZ * (i + 1))
+        out[k, 0, r] = w_y[cut] - slope[1][cut] * scale_z
+        out[k, 1, r] = slope[0][cut] * scale_z - w_x[cut]
+        out[k, 2, r] = spin_z[cut]
 
 
 def solution(mesh):
@@ -374,18 +381,17 @@
         z = sizes_of(mesh, whole, sketch_matrix.shape[1])
         S, PY, PZ, K, ZB, YB, XB, RY, RG, NX, NY, NZ = (z[n] for n in (
             "S", "PY", "PZ", "K", "ZB", "YB", "XB", "RY", "RG", "NX", "NY", "NZ"))
-        tables = tables_of(z)
-        my = jnp.broadcast_to(metric_y[:, None], (NY, LANES))
-        mz = jnp.broadcast_to(metric_z[:, None], (NZ, LANES))
+        tables, z_tables = tables_of(z)
         groups, fields = K * RG // 8, 7
         dma = pltpu.SemaphoreType.DMA
-        vmem = pl.BlockSpec(memory_space=pltpu.VMEM)
-        result = pl.pallas_call(
+        vmem, anywhere = pl.BlockSpec(memory_space=pltpu.VMEM), pl.BlockSpec(memory_space=pl.ANY)
+        lines = pl.pallas_call(
             functools.partial(body, z),
-            out_shape=jax.ShapeDtypeStruct((K, 3, RG, NZ, XB), F32),
-            in_specs=[pl.BlockSpec(memory_space=pl.ANY)] + [vmem] * 10 + [pl.BlockSpec(memory_space=pltpu.SMEM)],
-            out_specs=vmem,
-            scratch_shapes=[
+            out_shape=jax.ShapeDtypeStruct((groups * fields, 8 * NZ, XB), BF16),
+            in_specs=[anywhere] * 6 + [vmem] + [pl.BlockSpec(memory_space=pltpu.SMEM)] * 2,
+            out_specs=anywhere,
+            scratch_shapes=[pltpu.VMEM(t.shape, t.dtype) for t in tables] + [
+                pltpu.VMEM((RY, XB), F32),
                 pltpu.VMEM((2, ZB, YB, NX), BF16),
                 pltpu.VMEM((2 * ZB, YB, LANES), F32),
                 pltpu.VMEM((PY, YB, LANES), BF16),
@@ -400,17 +406,26 @@
                 pltpu.VMEM((2, K * RY, XB + LANES), BF16),
                 pltpu.VMEM((2, RY + 16, K * XB), BF16),
                 pltpu.VMEM((2, RY + 16, K * XB), BF16),
-                pltpu.VMEM((fields, 2 * K * RY, XB), BF16),
-                pltpu.VMEM((ZB // 2, PZ, groups * fields, 16, XB), BF16),
-                pltpu.VMEM((groups * fields, 8 * NZ, XB), BF16),
-                dma((ZB, PY - 1)), dma((ZB, PY - 1)), dma((PY - 1,)), dma((PY - 1,)),
-                dma((ZB, S - 1)), dma((ZB, S - 1)), dma((ZB, S - 1)), dma((ZB, S - 1)),
-                dma((S - 1,)), dma((S - 1,)), dma((ZB // 2, PZ - 1)), dma((ZB // 2, PZ - 1)),
-                dma((1,)), dma((ZB,)), dma((1,)), dma((ZB,)), dma((ZB,)), dma((1,)), dma((ZB // 2,)),
+                pltpu.VMEM((fields, K * RY, XB), BF16),
+                pltpu.VMEM((ZB, PZ, groups * fields, 8, XB), BF16),
+                dma((ZB, 3, PY - 1)), dma((ZB, 3, PY - 1)), dma((PY - 1,)), dma((PY - 1,)),
+                dma((ZB, 3, S - 1)), dma((ZB, 3, S - 1)), dma((ZB, S - 1)), dma((ZB, S - 1)),
+                dma((S - 1,)), dma((S - 1,)), dma((ZB, PZ - 1)), dma((ZB, PZ - 1)),
+                dma((5,)), dma((1,)), dma((ZB,)), dma((1,)), dma((ZB,)), dma((ZB,)), dma((1,)), dma((ZB,)),
             ],
             compiler_params=pltpu.CompilerParams(
-                collective_id=0, has_side_effects=True, vmem_limit_bytes=60 * 1024 * 1024),
-        )(velocity, *tables, metric_x[None, :], my, mz, sketch_matrix)
+                collective_id=0, has_side_effects=True, vmem_limit_bytes=56 * 1024 * 1024),
+        )(velocity, *tables, metric_x[None, :], metric_y, sketch_matrix.T)
+        per = 8 // K
+        whole_block = lambda t: pl.BlockSpec(t.shape, lambda g: (0,) * t.ndim)
+        metric_row = metric_z[None, :]
+        result = pl.pallas_call(
+            functools.partial(z_body, z),
+            grid=(groups,),
+            out_shape=jax.ShapeDtypeStruct((K, 3, RG, NZ, XB), F32),
+            in_specs=[pl.BlockSpec((fields, 8 * NZ, XB), lambda g: (g, 0, 0))] + [whole_block(t) for t in (*z_tables, metric_row)],
+            out_specs=pl.BlockSpec((K, 3, per, NZ, XB), lambda g: (0, 0, g, 0, 0)),
+        )(lines, *z_tables, metric_row)
         return jnp.swapaxes(result, 2, 3)
 
     return jax.shard_map(

time: 149 us -> 136 us (0.913); the launches traced: 147 us -> 136 us
  local copies, waits for them, and re-layouts: 8.2 us -> 0 us
  Pallas kernels: 139 us -> 136 us
    pallas_call x1, Pallas kernels: 139 us -> 129 us  [step(): pl.pallas_call(functools.partial(body, z), out_shape=jax.ShapeDtypeStruct...]
    pallas_call x0 -> x1, Pallas kernels: none -> 6.54 us  [step(): pl.pallas_call(functools.partial(z_body, z), grid=(groups,), out_shape=ja...]
    unnamed x2 -> x0, local copies, waits for them, and re-layouts: 5.41 us -> none
    broadcast_in_dim x2 -> x0, local copies, waits for them, and re-layouts: 2.79 us -> none  [the longest x1 1.47 us: step(): my = jnp.broadcast_to(metric_y[:, None], (NY, LANES))]
where the time goes in v2:
time: 136 us
  Pallas kernels  136 us (100%)
    pallas_call x1, Pallas kernels, step(): pl.pallas_call(functools.partial(body, z), out_shape=jax.ShapeDtypeStruct...  129 us
    pallas_call x1, Pallas kernels, step(): pl.pallas_call(functools.partial(z_body, z), grid=(groups,), out_shape=ja...  6.54 us

profile of v2, /device:TPU:1, one launch (start us, length us, event | category | flops | bytes accessed | tf_op | source)
XLA Modules:
  0.0 135.9 jit_solution(17881316238814526375)
XLA Ops:
  0.0 129.4 %shard_map.118.lines = bf16[21,384,256]{2,1,0:T(8,128)(2,1)} custom-call(bf16[1,3,6,96,1024]{4,3,2,1,0:T(8,128)(2,1)} %vel.1, bf16[2,1024,128]{2,1,0:T(8,128)(2,1)} %constant.14.clone.gx_in, bf16[2,64,384]{2,1,0:T(8,128)(2,1)} %constant.15.clone.gy_in, bf16[2,2,384,256]{3,2,1,0:T(8,128)(2,1)} %constant.16.clone.tx_in, ...), custom_call_target="tpu_custom_call" | custom-call | tf_op jit(solution)/shard_map/pallas_call | solution.py:388
  129.4 6.5 %shard_map.119 = f32[4,3,6,48,256]{4,3,2,1,0:T(8,128)} custom-call(bf16[21,384,256]{2,1,0:T(8,128)(2,1)} %shard_map.118.lines, bf16[2,384,384]{2,1,0:T(8,128)(2,1)} %constant.19.clone.dz, bf16[384,384]{1,0:T(8,128)(2,1)} %constant.23.turn, f32[1,48]{1,0:T(1,128)} %bitcast.6), custom_call_target="tpu_custom_call" | custom-call | tf_op jit(solution)/shard_map/pallas_call | solution.py:422

commit v3 on v2

--- a/solution.py
+++ b/solution.py
@@ -12,7 +12,7 @@
 F32 = jnp.float32
 BF16 = jnp.bfloat16
 LANES = 128
-NUMS = 8
+NUMS = 4
 
 
 def tridiagonal(n):
@@ -31,10 +31,9 @@
 
 def block_table(n):
     halo = np.zeros((n, NUMS))
-    halo[0, 0], halo[0, 1], halo[1, 1] = -1.0 / 36.0, -7.0 / 9.0, -1.0 / 36.0
-    halo[n - 1, 2], halo[n - 2, 2], halo[n - 1, 3] = 7.0 / 9.0, 1.0 / 36.0, 1.0 / 36.0
-    halo[0, 4:6] = -1.0 / 3.0
-    halo[n - 1, 6:8] = -1.0 / 3.0
+    edge = 7.0 / 9.0 + 1.0 / 36.0
+    halo[0, 0], halo[1, 0], halo[0, 1] = -edge, -1.0 / 36.0, 1.0
+    halo[n - 1, 2], halo[n - 2, 2], halo[n - 1, 3] = edge, 1.0 / 36.0, 1.0
     return np.linalg.solve(tridiagonal(n), np.concatenate([right_side(n), halo], axis=1))
 
 
@@ -44,13 +43,15 @@
     for block in range(blocks):
         low, high = block * size, (block + 1) * size
         if block > 0:
-            rows[block, 0, low - 2] = 1.0
-            rows[block, 1, low - 1] = 1.0
-            rows[block, 4] = rows[block, 5] = whole[low - 1]
+            rows[block, 0, low - 1] = 1.0
+            rows[block, 1] = -whole[low - 1] / 3.0
+            rows[block, 1, low - 1] += 1.0 / 36.0
+            rows[block, 1, low - 2] -= 1.0 / 36.0
         if block < blocks - 1:
             rows[block, 2, high] = 1.0
-            rows[block, 3, high + 1] = 1.0
-            rows[block, 6] = rows[block, 7] = whole[high]
+            rows[block, 3] = -whole[high] / 3.0
+            rows[block, 3, high + 1] += 1.0 / 36.0
+            rows[block, 3, high] -= 1.0 / 36.0
     return rows.reshape(blocks * NUMS, n)
 
 
@@ -82,7 +83,10 @@
     S, PY, PZ, K, RY, RG, XB, NZ = (z[n] for n in ("S", "PY", "PZ", "K", "RY", "RG", "XB", "NZ"))
     gx = np.zeros((z["NX"], LANES))
     gx[:, : PY * NUMS] = interface_rows(z["NX"], PY).T
-    gy = interface_rows(z["NY"], S)
+    numbers_y = interface_rows(z["NY"], S).reshape(S, NUMS, z["NY"])
+    gy = np.zeros((2, S, 2, NUMS, z["NY"]))
+    gy[0, :, 0] = gy[1, :, 1] = numbers_y
+    gy = gy.reshape(2, 2 * NUMS * S, z["NY"])
     bx, by = block_table(XB), block_table(RY)
     tx = np.zeros((2, XB + LANES, XB))
     ty = np.zeros((2, RY, RY + 16))
@@ -105,8 +109,8 @@
 
 
 def body(
-    z, vel, gx_in, gy_in, tx_in, ty_in, gather_in, mx, my, sk, out,
-    gx, gy, tx, ty, gather, scale_y,
+    z, vel, gx_in, gy_in, tx_in, ty_in, gather_in, mx_in, my_in, sk_in, out,
+    gx, gy, tx, ty, gather, mx, my, sk, scale_y,
     vw, ef, es, buf_a, buf_e, buf_y, buf_c, buf_cy, buf_ce, se, xh, xl, yh, yl, pb, buf_bs,
     send_a, recv_a, send_e, recv_e, send_c, recv_c, send_cy, recv_cy, send_ce, recv_ce, send_b, recv_b,
     local_t, local_v, local_a, local_e, local_c, local_cy, local_ce, local_b,
@@ -166,13 +170,16 @@
     def b_rows(p):
         return pl.ds(pl.multiple_of((me_z * ZB + p) * 8, 8), 8)
 
-    def b_copy(p, d):
+    part_of = (slice(0, 5), slice(5, 7))
+
+    def b_copy(p, part, d):
         peer = other(me_z, d, PZ)
-        return remote(buf_bs.at[p, peer], out.at[:, b_rows(p), :],
-                      send_b.at[p, d - 1], recv_b.at[p, d - 1], "pz", peer)
-
-    def b_local(p):
-        return pltpu.make_async_copy(buf_bs.at[p, me_z], out.at[:, b_rows(p), :], local_b.at[p])
+        return remote(buf_bs.at[p, peer, part_of[part]], out.at[part_of[part], :, b_rows(p), :],
+                      send_b.at[p, part, d - 1], recv_b.at[p, part, d - 1], "pz", peer)
+
+    def b_local(p, part):
+        return pltpu.make_async_copy(
+            buf_bs.at[p, me_z, part_of[part]], out.at[part_of[part], :, b_rows(p), :], local_b.at[p, part])
 
     barrier = pltpu.get_barrier_semaphore()
     for axis, me, n in (("py", me_y, PY), ("snap", me_s, S), ("pz", me_z, PZ)):
@@ -180,21 +187,24 @@
             pl.semaphore_signal(barrier, inc=1, device_id={axis: other(me, d, n)}, device_id_type=MESH)
     pl.semaphore_wait(barrier, PY + S + PZ - 3)
 
-    for p in range(ZB):
+    def a_start(p):
         for f in range(3):
             for d in range(1, PY):
                 a_copy(p, f, d).start()
         a_local(p).start()
+
+    lag = min(3, ZB)
+    for p in range(lag):
+        a_start(p)
     planes_in = pltpu.make_async_copy(vel.at[0, 1:3], vw, local_v.at[0])
     planes_in.start()
-    tables = [
-        pltpu.make_async_copy(src, dst, local_t.at[t])
-        for t, (src, dst) in enumerate(((gx_in, gx), (gy_in, gy), (tx_in, tx), (ty_in, ty), (gather_in, gather)))
-    ]
+    pairs = ((gx_in, gx), (my_in, my), (gy_in, gy), (sk_in, sk), (tx_in, tx), (ty_in, ty), (gather_in, gather),
+             (mx_in.at[:, mult(me_y, XB)], mx))
+    tables = [pltpu.make_async_copy(src, dst, local_t.at[t]) for t, (src, dst) in enumerate(pairs)]
     for table in tables:
         table.start()
-    for r in range(RY):
-        scale_y[r : r + 1, :] = jnp.full((1, XB), my[me_s * RY + r], F32)
+    for part in (yh, yl):
+        part[:, RY + 2 * NUMS :, :] = jnp.zeros((2, 16 - 2 * NUMS, K * XB), BF16)
 
     planes_in.wait()
     tables[0].wait()
@@ -209,36 +219,35 @@
         for j in range(2 * ZB):
             shifted = pltpu.roll(ef[j], (NUMS * (j - b)) % LANES, 1)
             total = jnp.where((lane >= NUMS * j) & (lane < NUMS * (j + 1)), shifted, total)
-        rounded = total.astype(BF16).astype(F32)
-        low = (lane % NUMS == 5) | (lane % NUMS == 7)
-        es[b] = jnp.where(low, total - rounded, rounded).astype(BF16)
+        es[b] = total.astype(BF16)
     for d in range(1, PY):
         e_copy(d).start()
     e_local().start()
 
+    for p in range(lag, ZB):
+        a_start(p)
     tables[1].wait()
+    for r in range(RY):
+        scale_y[r : r + 1, :] = jnp.full((1, XB), my[me_s * RY + r], F32)
+    tables[2].wait()
 
     def a_stage(p):
         a_local(p).wait()
         for f in range(3):
             for d in range(1, PY):
                 a_copy(p, f, d).wait_recv()
-            for d in range(1, S):
-                c_copy(p, f, d).start()
+            if f < 2:
+                for d in range(1, S):
+                    c_copy(p, f, d).start()
+        numbers = (dot(gy[0, 0], buf_a[p, 0]) + dot(gy[1, 0], buf_a[p, 0])) + (
+            dot(gy[0, 1], buf_a[p, 2]) + dot(gy[1, 1], buf_a[p, 2]))
+        for s in range(S):
+            buf_y[p, s] = numbers[2 * NUMS * s : 2 * NUMS * (s + 1)].astype(BF16)
+        for d in range(1, S):
+            cy_copy(p, d).start()
+        for d in range(1, S):
+            c_copy(p, 2, d).start()
         c_local(p).start()
-        row = lax.broadcasted_iota(jnp.int32, (S * NUMS, XB), 0)
-        low = (row % NUMS == 5) | (row % NUMS == 7)
-        parts = []
-        for f in (0, 2):
-            field = buf_a[p, f]
-            numbers = dot(gy[0], field) + dot(gy[1], field)
-            rounded = numbers.astype(BF16).astype(F32)
-            parts.append(jnp.where(low, numbers - rounded, rounded))
-        for s in range(S):
-            cut = slice(NUMS * s, NUMS * (s + 1))
-            buf_y[p, s] = jnp.concatenate([parts[0][cut], parts[1][cut]], axis=0).astype(BF16)
-        for d in range(1, S):
-            cy_copy(p, d).start()
         cy_local(p).start()
 
     def e_stage():
@@ -250,7 +259,7 @@
         ce_local().start()
 
     def se_stage():
-        for table in tables[2:]:
+        for table in tables[3:]:
             table.wait()
         ce_local().wait()
         for d in range(1, S):
@@ -261,66 +270,81 @@
                 total = total + sk[k, s] * buf_ce[s].astype(F32)
             se[RY * k : RY * (k + 1), :] = total
 
+    def sketch(parts, k):
+        total = sk[k, 0] * parts[0]
+        for s in range(1, S):
+            total = total + sk[k, s] * parts[s]
+        return halves(total)
+
+    def sketch_field(p, f):
+        for t in range(RY // 16):
+            rows = slice(16 * t, 16 * (t + 1))
+            parts = [buf_c[s, p, f, rows, :].astype(F32) for s in range(S)]
+            for k in range(K):
+                high, low = sketch(parts, k)
+                own = slice(RY * k + 16 * t, RY * k + 16 * (t + 1))
+                if f != 1:
+                    yh[f // 2, rows, XB * k : XB * (k + 1)] = high
+                    yl[f // 2, rows, XB * k : XB * (k + 1)] = low
+                if f != 0:
+                    xh[f - 1, own, :XB] = high
+                    xl[f - 1, own, :XB] = low
+                if f != 2:
+                    pb[2 * f, own, :] = high
+                    pb[2 * f + 1, own, :] = low
+
+    def x_slope(f):
+        return dot(xh[f], tx[0, f]) + dot(xl[f], tx[0, f]) + dot(xh[f], tx[1, f])
+
+    def y_slope(f):
+        return dot(ty[0, f], yh[f]) + dot(ty[0, f], yl[f]) + dot(ty[1, f], yh[f])
+
+    def send_part(p, part):
+        for f in range(part_of[part].start, part_of[part].stop):
+            moved = dot(gather[...], pb[f]).astype(BF16)
+            for q in range(PZ):
+                for g in range(groups):
+                    cut = (q * groups + g) * 8
+                    buf_bs[p, q, f, g] = moved[cut : cut + 8]
+        for d in range(1, PZ):
+            b_copy(p, part, d).start()
+        b_local(p, part).start()
+
     def s_stage(p):
         c_local(p).wait()
         cy_local(p).wait()
         for d in range(1, S):
-            for f in range(3):
-                c_copy(p, f, d).wait_recv()
+            c_copy(p, 0, d).wait_recv()
+            c_copy(p, 1, d).wait_recv()
             cy_copy(p, d).wait_recv()
-
-        def sketch(parts, k):
-            total = sk[k, 0] * parts[0]
-            for s in range(1, S):
-                total = total + sk[k, s] * parts[s]
-            return halves(total)
-
-        for f in range(3):
-            for t in range(RY // 16):
-                rows = slice(16 * t, 16 * (t + 1))
-                parts = [buf_c[s, p, f, rows, :].astype(F32) for s in range(S)]
-                for k in range(K):
-                    high, low = sketch(parts, k)
-                    if f != 1:
-                        yh[f // 2, rows, XB * k : XB * (k + 1)] = high
-                        yl[f // 2, rows, XB * k : XB * (k + 1)] = low
-                    own = slice(RY * k + 16 * t, RY * k + 16 * (t + 1))
-                    if f != 0:
-                        xh[f - 1, own, :XB] = high
-                        xl[f - 1, own, :XB] = low
-                    if f != 2:
-                        pb[2 * f, own, :] = high
-                        pb[2 * f + 1, own, :] = low
+        sketch_field(p, 0)
+        sketch_field(p, 1)
         parts = [buf_cy[s, p].astype(F32) for s in range(S)]
         for k in range(K):
             high, low = sketch(parts, k)
             for f in range(2):
-                yh[f, RY : RY + 16, XB * k : XB * (k + 1)] = high
-                yl[f, RY : RY + 16, XB * k : XB * (k + 1)] = low
+                yh[f, RY : RY + 2 * NUMS, XB * k : XB * (k + 1)] = high
+                yl[f, RY : RY + 2 * NUMS, XB * k : XB * (k + 1)] = low
         high, low = halves(pltpu.roll(se[...], lax.rem(LANES - 2 * NUMS * p, LANES), 1))
         for f in range(2):
             xh[f, :, XB:] = high
             xl[f, :, XB:] = low
-
-        x_slopes = [dot(xh[f], tx[0, f]) + dot(xl[f], tx[0, f]) + dot(xh[f], tx[1, f]) for f in range(2)]
-        y_slopes = [dot(ty[0, f], yh[f]) + dot(ty[0, f], yl[f]) + dot(ty[1, f], yh[f]) for f in range(2)]
-        scale_x = mx[0:1, mult(me_y, XB)]
+        scale_x = mx[...]
+        x_slopes, y_slopes = x_slope(0), y_slope(0)
         for k in range(K):
             own, cols = slice(RY * k, RY * (k + 1)), slice(XB * k, XB * (k + 1))
-            pb[4, own, :] = (x_slopes[1][own] * scale_x).astype(BF16)
-            pb[5, own, :] = (y_slopes[1][:, cols] * scale_y[...]).astype(BF16)
-            pb[6, own, :] = (x_slopes[0][own] * scale_x - y_slopes[0][:, cols] * scale_y[...]).astype(BF16)
-        for f in range(fields):
-            moved = dot(gather[...], pb[f]).astype(BF16)
-            for q in range(PZ):
-                for g in range(groups):
-                    cut = (q * groups + g) * 8
-                    buf_bs[p, q, g * fields + f] = moved[cut : cut + 8]
-        for d in range(1, PZ):
-            b_copy(p, d).start()
-        b_local(p).start()
-
-    lag = min(3, ZB)
+            pb[4, own, :] = (x_slopes[own] * scale_x - y_slopes[:, cols] * scale_y[...]).astype(BF16)
+        send_part(p, 0)
+
+        for d in range(1, S):
+            c_copy(p, 2, d).wait_recv()
+        sketch_field(p, 2)
+        x_slopes, y_slopes = x_slope(1), y_slope(1)
+        for k in range(K):
+            own, cols = slice(RY * k, RY * (k + 1)), slice(XB * k, XB * (k + 1))
+            pb[5, own, :] = (x_slopes[own] * scale_x).astype(BF16)
+            pb[6, own, :] = (y_slopes[:, cols] * scale_y[...]).astype(BF16)
+        send_part(p, 1)
 
     @pl.loop(0, ZB + lag)
     def _(i):
@@ -328,7 +352,7 @@
         def _():
             a_stage(i)
 
-        @pl.when(i == 1)
+        @pl.when(i == lag - 1)
         def _():
             e_stage()
 
@@ -341,9 +365,10 @@
             s_stage(i - lag)
 
     for p in range(ZB):
-        b_local(p).wait()
-        for d in range(1, PZ):
-            b_copy(p, d).wait_recv()
+        for part in range(2):
+            b_local(p, part).wait()
+            for d in range(1, PZ):
+                b_copy(p, part, d).wait_recv()
 
     for p in range(ZB):
         for f in range(3):
@@ -353,8 +378,9 @@
                 c_copy(p, f, d).wait_send()
         for d in range(1, S):
             cy_copy(p, d).wait_send()
-        for d in range(1, PZ):
-            b_copy(p, d).wait_send()
+        for part in range(2):
+            for d in range(1, PZ):
+                b_copy(p, part, d).wait_send()
     for d in range(1, PY):
         e_copy(d).wait_send()
     for d in range(1, S):
@@ -366,7 +392,7 @@
     same = lax.broadcasted_iota(jnp.int32, (NZ, NZ), 0) == lax.broadcasted_iota(jnp.int32, (NZ, NZ), 1)
     scale_z = jnp.broadcast_to(jnp.sum(jnp.where(same, mz[...], 0.0), axis=1, keepdims=True), (NZ, XB))
     slope = [dot(dz[0], lines[2 * f]) + dot(dz[0], lines[2 * f + 1]) + dot(dz[1], lines[2 * f]) for f in range(2)]
-    w_x, w_y, spin_z = (dot(turn[...], lines[f]) for f in (4, 5, 6))
+    w_x, w_y, spin_z = (dot(turn[...], lines[f]) for f in (5, 6, 4))
     for i in range(8):
         r, k = divmod(i, K)
         cut = slice(NZ * i, NZ * (i + 1))
@@ -384,22 +410,25 @@
         tables, z_tables = tables_of(z)
         groups, fields = K * RG // 8, 7
         dma = pltpu.SemaphoreType.DMA
-        vmem, anywhere = pl.BlockSpec(memory_space=pltpu.VMEM), pl.BlockSpec(memory_space=pl.ANY)
+        anywhere = pl.BlockSpec(memory_space=pl.ANY)
         lines = pl.pallas_call(
             functools.partial(body, z),
-            out_shape=jax.ShapeDtypeStruct((groups * fields, 8 * NZ, XB), BF16),
-            in_specs=[anywhere] * 6 + [vmem] + [pl.BlockSpec(memory_space=pltpu.SMEM)] * 2,
+            out_shape=jax.ShapeDtypeStruct((fields, groups, 8 * NZ, XB), BF16),
+            in_specs=[anywhere] * 9,
             out_specs=anywhere,
             scratch_shapes=[pltpu.VMEM(t.shape, t.dtype) for t in tables] + [
+                pltpu.VMEM((1, XB), F32),
+                pltpu.SMEM((NY,), F32),
+                pltpu.SMEM((K, S), F32),
                 pltpu.VMEM((RY, XB), F32),
                 pltpu.VMEM((2, ZB, YB, NX), BF16),
                 pltpu.VMEM((2 * ZB, YB, LANES), F32),
                 pltpu.VMEM((PY, YB, LANES), BF16),
                 pltpu.VMEM((ZB, 3, NY, XB), BF16),
                 pltpu.VMEM((NY, LANES), BF16),
-                pltpu.VMEM((ZB, S, 16, XB), BF16),
+                pltpu.VMEM((ZB, S, 2 * NUMS, XB), BF16),
                 pltpu.VMEM((S, ZB, 3, RY, XB), BF16),
-                pltpu.VMEM((S, ZB, 16, XB), BF16),
+                pltpu.VMEM((S, ZB, 2 * NUMS, XB), BF16),
                 pltpu.VMEM((S, RY, LANES), BF16),
                 pltpu.VMEM((K * RY, LANES), F32),
                 pltpu.VMEM((2, K * RY, XB + LANES), BF16),
@@ -407,11 +436,11 @@
                 pltpu.VMEM((2, RY + 16, K * XB), BF16),
                 pltpu.VMEM((2, RY + 16, K * XB), BF16),
                 pltpu.VMEM((fields, K * RY, XB), BF16),
-                pltpu.VMEM((ZB, PZ, groups * fields, 8, XB), BF16),
+                pltpu.VMEM((ZB, PZ, fields, groups, 8, XB), BF16),
                 dma((ZB, 3, PY - 1)), dma((ZB, 3, PY - 1)), dma((PY - 1,)), dma((PY - 1,)),
                 dma((ZB, 3, S - 1)), dma((ZB, 3, S - 1)), dma((ZB, S - 1)), dma((ZB, S - 1)),
-                dma((S - 1,)), dma((S - 1,)), dma((ZB, PZ - 1)), dma((ZB, PZ - 1)),
-                dma((5,)), dma((1,)), dma((ZB,)), dma((1,)), dma((ZB,)), dma((ZB,)), dma((1,)), dma((ZB,)),
+                dma((S - 1,)), dma((S - 1,)), dma((ZB, 2, PZ - 1)), dma((ZB, 2, PZ - 1)),
+                dma((8,)), dma((1,)), dma((ZB,)), dma((1,)), dma((ZB,)), dma((ZB,)), dma((1,)), dma((ZB, 2)),
             ],
             compiler_params=pltpu.CompilerParams(
                 collective_id=0, has_side_effects=True, vmem_limit_bytes=56 * 1024 * 1024),
@@ -423,7 +452,7 @@
             functools.partial(z_body, z),
             grid=(groups,),
             out_shape=jax.ShapeDtypeStruct((K, 3, RG, NZ, XB), F32),
-            in_specs=[pl.BlockSpec((fields, 8 * NZ, XB), lambda g: (g, 0, 0))] + [whole_block(t) for t in (*z_tables, metric_row)],
+            in_specs=[pl.BlockSpec((fields, pl.Squeezed(), 8 * NZ, XB), lambda g: (0, g, 0, 0))] + [whole_block(t) for t in (*z_tables, metric_row)],
             out_specs=pl.BlockSpec((K, 3, per, NZ, XB), lambda g: (0, 0, g, 0, 0)),
         )(lines, *z_tables, metric_row)
         return jnp.swapaxes(result, 2, 3)

time: 136 us -> 122 us (0.90)
  Pallas kernels: 136 us -> 121 us
    pallas_call x1, Pallas kernels: 129 us -> 115 us  [step(): pl.pallas_call(functools.partial(body, z), out_shape=jax.ShapeDtypeStruct...]
where the time goes in v3:
time: 122 us
  Pallas kernels  121 us (99%)
    pallas_call x1, Pallas kernels, step(): pl.pallas_call(functools.partial(body, z), out_shape=jax.ShapeDtypeStruct...  115 us
    pallas_call x1, Pallas kernels, step(): pl.pallas_call(functools.partial(z_body, z), grid=(groups,), out_shape=ja...  6.55 us

profile of v3, /device:TPU:1, one launch (start us, length us, event | category | flops | bytes accessed | tf_op | source)
XLA Modules:
  0.0 121.5 jit_solution(1282040241039927713)
XLA Ops:
  0.0 114.9 %shard_map.118.lines = bf16[7,3,384,256]{3,2,1,0:T(8,128)(2,1)} custom-call(bf16[1,3,6,96,1024]{4,3,2,1,0:T(8,128)(2,1)} %vel.1, bf16[2,1024,128]{2,1,0:T(8,128)(2,1)} %constant.14.clone.gx_in, bf16[2,2,64,384]{3,2,1,0:T(8,128)(2,1)} %constant.15.clone.gy_in, bf16[2,2,384,256]{3,2,1,0:T(8,128)(2,1)} %constant.16.clone.tx_in, ...), custom_call_target="tpu_custom_call" | custom-call | tf_op jit(solution)/shard_map/pallas_call | solution.py:414
  115.0 6.6 %shard_map.119 = f32[4,3,6,48,256]{4,3,2,1,0:T(8,128)} custom-call(bf16[7,3,384,256]{3,2,1,0:T(8,128)(2,1)} %shard_map.118.lines, bf16[2,384,384]{2,1,0:T(8,128)(2,1)} %constant.19.clone.dz, bf16[384,384]{1,0:T(8,128)(2,1)} %constant.23.turn, f32[1,48]{1,0:T(1,128)} %bitcast.6), custom_call_target="tpu_custom_call" | custom-call | tf_op jit(solution)/shard_map/pallas_call | solution.py:451

commit v4 on v3

--- a/solution.py
+++ b/solution.py
@@ -68,6 +68,10 @@
 def halves(value):
     high = value.astype(BF16)
     return high, (value - high.astype(F32)).astype(BF16)
+
+
+def far_first(n):
+    return sorted(range(1, n), key=lambda d: -min(d, n - d))
 
 
 def sizes_of(mesh, shape, rank):
@@ -111,12 +115,12 @@
 def body(
     z, vel, gx_in, gy_in, tx_in, ty_in, gather_in, mx_in, my_in, sk_in, out,
     gx, gy, tx, ty, gather, mx, my, sk, scale_y,
-    vw, ef, es, buf_a, buf_e, buf_y, buf_c, buf_cy, buf_ce, se, xh, xl, yh, yl, pb, buf_bs,
-    send_a, recv_a, send_e, recv_e, send_c, recv_c, send_cy, recv_cy, send_ce, recv_ce, send_b, recv_b,
-    local_t, local_v, local_a, local_e, local_c, local_cy, local_ce, local_b,
+    vw, ef, es, buf_a, buf_v, buf_e, buf_c, buf_cv, buf_ce, se, xh, xl, yh, yl, pb, buf_bs,
+    send_a, recv_a, send_e, recv_e, send_c, recv_c, send_ce, recv_ce, send_b, recv_b,
+    local_t, local_v, local_a, local_e, local_c, local_ce, local_b,
 ):
     S, PY, PZ, K, ZB, YB, XB, RY, RG = (z[n] for n in ("S", "PY", "PZ", "K", "ZB", "YB", "XB", "RY", "RG"))
-    groups, fields = K * RG // 8, 7
+    groups, H = K * RG // 8, YB // RY
     me_s, me_y, me_z = lax.axis_index("snap"), lax.axis_index("py"), lax.axis_index("pz")
 
     def other(me, d, n):
@@ -129,43 +133,43 @@
     def mult(value, size):
         return pl.ds(pl.multiple_of(value * size, size), size)
 
+    def a_ends(p, f, peer):
+        own = pl.ds(me_y * H, H)
+        dst = buf_v.at[p, own, :RY, :] if f == 1 else buf_a.at[p, f // 2, own]
+        return vel.at[0, f, p, :, :, mult(peer, XB)], dst
+
     def a_copy(p, f, d):
         peer = other(me_y, d, PY)
-        return remote(vel.at[0, f, p, :, mult(peer, XB)], buf_a.at[p, f, mult(me_y, YB), :],
-                      send_a.at[p, f, d - 1], recv_a.at[p, f, d - 1], "py", peer)
-
-    def a_local(p):
-        return pltpu.make_async_copy(vel.at[0, :, p, :, mult(me_y, XB)], buf_a.at[p, :, mult(me_y, YB), :], local_a.at[p])
+        return remote(*a_ends(p, f, peer), send_a.at[p, f, d - 1], recv_a.at[p, f, d - 1], "py", peer)
+
+    def a_local(p, f):
+        return pltpu.make_async_copy(*a_ends(p, f, me_y), local_a.at[p, f])
 
     def e_copy(d):
         peer = other(me_y, d, PY)
-        return remote(es.at[peer], buf_e.at[mult(me_y, YB), :], send_e.at[d - 1], recv_e.at[d - 1], "py", peer)
+        return remote(es.at[peer], buf_e.at[mult(me_y, YB // 2), :], send_e.at[d - 1], recv_e.at[d - 1], "py", peer)
 
     def e_local():
-        return pltpu.make_async_copy(es.at[me_y], buf_e.at[mult(me_y, YB), :], local_e.at[0])
+        return pltpu.make_async_copy(es.at[me_y], buf_e.at[mult(me_y, YB // 2), :], local_e.at[0])
+
+    def c_ends(p, f, peer):
+        if f == 1:
+            return buf_v.at[p, peer], buf_cv.at[me_s, p]
+        return buf_a.at[p, f // 2, peer], buf_c.at[me_s, p, f // 2]
 
     def c_copy(p, f, d):
         peer = other(me_s, d, S)
-        return remote(buf_a.at[p, f, mult(peer, RY), :], buf_c.at[me_s, p, f],
-                      send_c.at[p, f, d - 1], recv_c.at[p, f, d - 1], "snap", peer)
-
-    def c_local(p):
-        return pltpu.make_async_copy(buf_a.at[p, :, mult(me_s, RY), :], buf_c.at[me_s, p], local_c.at[p])
-
-    def cy_copy(p, d):
-        peer = other(me_s, d, S)
-        return remote(buf_y.at[p, peer], buf_cy.at[me_s, p],
-                      send_cy.at[p, d - 1], recv_cy.at[p, d - 1], "snap", peer)
-
-    def cy_local(p):
-        return pltpu.make_async_copy(buf_y.at[p, me_s], buf_cy.at[me_s, p], local_cy.at[p])
+        return remote(*c_ends(p, f, peer), send_c.at[p, f, d - 1], recv_c.at[p, f, d - 1], "snap", peer)
+
+    def c_local(p, f):
+        return pltpu.make_async_copy(*c_ends(p, f, me_s), local_c.at[p, f])
 
     def ce_copy(d):
         peer = other(me_s, d, S)
-        return remote(buf_e.at[mult(peer, RY), :], buf_ce.at[me_s], send_ce.at[d - 1], recv_ce.at[d - 1], "snap", peer)
+        return remote(buf_e.at[mult(peer, RY // 2), :], buf_ce.at[me_s], send_ce.at[d - 1], recv_ce.at[d - 1], "snap", peer)
 
     def ce_local():
-        return pltpu.make_async_copy(buf_e.at[mult(me_s, RY), :], buf_ce.at[me_s], local_ce.at[0])
+        return pltpu.make_async_copy(buf_e.at[mult(me_s, RY // 2), :], buf_ce.at[me_s], local_ce.at[0])
 
     def b_rows(p):
         return pl.ds(pl.multiple_of((me_z * ZB + p) * 8, 8), 8)
@@ -188,10 +192,10 @@
     pl.semaphore_wait(barrier, PY + S + PZ - 3)
 
     def a_start(p):
-        for f in range(3):
-            for d in range(1, PY):
+        for f in (0, 2, 1):
+            for d in far_first(PY):
                 a_copy(p, f, d).start()
-        a_local(p).start()
+            a_local(p, f).start()
 
     lag = min(3, ZB)
     for p in range(lag):
@@ -212,15 +216,19 @@
     for f in range(2):
         for p in range(ZB):
             j = 2 * p + f
-            line = vw[f, p]
+            line = vw[f, p].reshape(YB, z["NX"])
             ef[j] = dot(line, gx[0]) + dot(line, gx[1])
     for b in range(PY):
         total = jnp.zeros((YB, LANES), F32)
         for j in range(2 * ZB):
             shifted = pltpu.roll(ef[j], (NUMS * (j - b)) % LANES, 1)
             total = jnp.where((lane >= NUMS * j) & (lane < NUMS * (j + 1)), shifted, total)
-        es[b] = total.astype(BF16)
-    for d in range(1, PY):
+        half = RY // 2
+        for h in range(H):
+            upper, lower = total[RY * h : RY * h + half], total[RY * h + half : RY * (h + 1)]
+            both = jnp.where(lane[:half] < LANES // 2, upper, pltpu.roll(lower, LANES // 2, 1))
+            es[b, half * h : half * (h + 1), :] = both.astype(BF16)
+    for d in far_first(PY):
         e_copy(d).start()
     e_local().start()
 
@@ -231,30 +239,32 @@
         scale_y[r : r + 1, :] = jnp.full((1, XB), my[me_s * RY + r], F32)
     tables[2].wait()
 
+    def arrived(p, f):
+        a_local(p, f).wait()
+        for d in far_first(PY):
+            a_copy(p, f, d).wait_recv()
+
+    def go_on(p, f):
+        for d in far_first(S):
+            c_copy(p, f, d).start()
+        c_local(p, f).start()
+
     def a_stage(p):
-        a_local(p).wait()
-        for f in range(3):
-            for d in range(1, PY):
-                a_copy(p, f, d).wait_recv()
-            if f < 2:
-                for d in range(1, S):
-                    c_copy(p, f, d).start()
-        numbers = (dot(gy[0, 0], buf_a[p, 0]) + dot(gy[1, 0], buf_a[p, 0])) + (
-            dot(gy[0, 1], buf_a[p, 2]) + dot(gy[1, 1], buf_a[p, 2]))
+        arrived(p, 0)
+        go_on(p, 0)
+        arrived(p, 2)
+        vel_u, vel_w = (buf_a[p, f].reshape(z["NY"], XB) for f in range(2))
+        numbers = (dot(gy[0, 0], vel_u) + dot(gy[1, 0], vel_u)) + (dot(gy[0, 1], vel_w) + dot(gy[1, 1], vel_w))
         for s in range(S):
-            buf_y[p, s] = numbers[2 * NUMS * s : 2 * NUMS * (s + 1)].astype(BF16)
-        for d in range(1, S):
-            cy_copy(p, d).start()
-        for d in range(1, S):
-            c_copy(p, 2, d).start()
-        c_local(p).start()
-        cy_local(p).start()
+            buf_v[p, s, RY:, :] = numbers[2 * NUMS * s : 2 * NUMS * (s + 1)].astype(BF16)
+        arrived(p, 1)
+        go_on(p, 1)
 
     def e_stage():
         e_local().wait()
-        for d in range(1, PY):
+        for d in far_first(PY):
             e_copy(d).wait_recv()
-        for d in range(1, S):
+        for d in far_first(S):
             ce_copy(d).start()
         ce_local().start()
 
@@ -262,13 +272,14 @@
         for table in tables[3:]:
             table.wait()
         ce_local().wait()
-        for d in range(1, S):
+        for d in far_first(S):
             ce_copy(d).wait_recv()
         for k in range(K):
             total = sk[k, 0] * buf_ce[0].astype(F32)
             for s in range(1, S):
                 total = total + sk[k, s] * buf_ce[s].astype(F32)
-            se[RY * k : RY * (k + 1), :] = total
+            se[RY * k : RY * k + RY // 2, :] = total
+            se[RY * k + RY // 2 : RY * (k + 1), :] = pltpu.roll(total, LANES // 2, 1)
 
     def sketch(parts, k):
         total = sk[k, 0] * parts[0]
@@ -279,7 +290,7 @@
     def sketch_field(p, f):
         for t in range(RY // 16):
             rows = slice(16 * t, 16 * (t + 1))
-            parts = [buf_c[s, p, f, rows, :].astype(F32) for s in range(S)]
+            parts = [(buf_cv[s, p, rows, :] if f == 1 else buf_c[s, p, f // 2, rows, :]).astype(F32) for s in range(S)]
             for k in range(K):
                 high, low = sketch(parts, k)
                 own = slice(RY * k + 16 * t, RY * k + 16 * (t + 1))
@@ -306,52 +317,58 @@
                 for g in range(groups):
                     cut = (q * groups + g) * 8
                     buf_bs[p, q, f, g] = moved[cut : cut + 8]
-        for d in range(1, PZ):
+        for d in far_first(PZ):
             b_copy(p, part, d).start()
         b_local(p, part).start()
 
-    def s_stage(p):
-        c_local(p).wait()
-        cy_local(p).wait()
-        for d in range(1, S):
-            c_copy(p, 0, d).wait_recv()
-            c_copy(p, 1, d).wait_recv()
-            cy_copy(p, d).wait_recv()
-        sketch_field(p, 0)
-        sketch_field(p, 1)
-        parts = [buf_cy[s, p].astype(F32) for s in range(S)]
+    def sketch_numbers(p, f):
+        parts = [buf_cv[s, p, RY:, :].astype(F32) for s in range(S)]
         for k in range(K):
             high, low = sketch(parts, k)
-            for f in range(2):
-                yh[f, RY : RY + 2 * NUMS, XB * k : XB * (k + 1)] = high
-                yl[f, RY : RY + 2 * NUMS, XB * k : XB * (k + 1)] = low
+            yh[f, RY : RY + 2 * NUMS, XB * k : XB * (k + 1)] = high
+            yl[f, RY : RY + 2 * NUMS, XB * k : XB * (k + 1)] = low
         high, low = halves(pltpu.roll(se[...], lax.rem(LANES - 2 * NUMS * p, LANES), 1))
-        for f in range(2):
-            xh[f, :, XB:] = high
-            xl[f, :, XB:] = low
-        scale_x = mx[...]
+        xh[f, :, XB:] = high
+        xl[f, :, XB:] = low
+
+    def came(p, f):
+        c_local(p, f).wait()
+        for d in far_first(S):
+            c_copy(p, f, d).wait_recv()
+
+    def uv_stage(p):
+        came(p, 0)
+        sketch_field(p, 0)
+        came(p, 1)
+        sketch_field(p, 1)
+        sketch_numbers(p, 0)
         x_slopes, y_slopes = x_slope(0), y_slope(0)
         for k in range(K):
             own, cols = slice(RY * k, RY * (k + 1)), slice(XB * k, XB * (k + 1))
-            pb[4, own, :] = (x_slopes[own] * scale_x - y_slopes[:, cols] * scale_y[...]).astype(BF16)
+            pb[4, own, :] = (x_slopes[own] * mx[...] - y_slopes[:, cols] * scale_y[...]).astype(BF16)
         send_part(p, 0)
 
-        for d in range(1, S):
-            c_copy(p, 2, d).wait_recv()
+    def w_stage(p):
+        came(p, 2)
         sketch_field(p, 2)
+        sketch_numbers(p, 1)
         x_slopes, y_slopes = x_slope(1), y_slope(1)
         for k in range(K):
             own, cols = slice(RY * k, RY * (k + 1)), slice(XB * k, XB * (k + 1))
-            pb[5, own, :] = (x_slopes[own] * scale_x).astype(BF16)
+            pb[5, own, :] = (x_slopes[own] * mx[...]).astype(BF16)
             pb[6, own, :] = (y_slopes[:, cols] * scale_y[...]).astype(BF16)
         send_part(p, 1)
 
-    @pl.loop(0, ZB + lag)
+    @pl.loop(0, ZB + lag + 1)
     def _(i):
         @pl.when(i < ZB)
         def _():
             a_stage(i)
 
+        @pl.when((i >= 1) & (i <= ZB))
+        def _():
+            go_on(i - 1, 2)
+
         @pl.when(i == lag - 1)
         def _():
             e_stage()
@@ -360,30 +377,32 @@
         def _():
             se_stage()
 
-        @pl.when(i >= lag)
-        def _():
-            s_stage(i - lag)
+        @pl.when((i >= lag) & (i < ZB + lag))
+        def _():
+            uv_stage(i - lag)
+
+        @pl.when(i > lag)
+        def _():
+            w_stage(i - lag - 1)
 
     for p in range(ZB):
         for part in range(2):
             b_local(p, part).wait()
-            for d in range(1, PZ):
+            for d in far_first(PZ):
                 b_copy(p, part, d).wait_recv()
 
     for p in range(ZB):
         for f in range(3):
-            for d in range(1, PY):
+            for d in far_first(PY):
                 a_copy(p, f, d).wait_send()
-            for d in range(1, S):
+            for d in far_first(S):
                 c_copy(p, f, d).wait_send()
-        for d in range(1, S):
-            cy_copy(p, d).wait_send()
         for part in range(2):
-            for d in range(1, PZ):
+            for d in far_first(PZ):
                 b_copy(p, part, d).wait_send()
-    for d in range(1, PY):
+    for d in far_first(PY):
         e_copy(d).wait_send()
-    for d in range(1, S):
+    for d in far_first(S):
         ce_copy(d).wait_send()
 
 
@@ -421,15 +440,15 @@
                 pltpu.SMEM((NY,), F32),
                 pltpu.SMEM((K, S), F32),
                 pltpu.VMEM((RY, XB), F32),
-                pltpu.VMEM((2, ZB, YB, NX), BF16),
+                pltpu.VMEM((2, ZB, YB // RY, RY, NX), BF16),
                 pltpu.VMEM((2 * ZB, YB, LANES), F32),
-                pltpu.VMEM((PY, YB, LANES), BF16),
-                pltpu.VMEM((ZB, 3, NY, XB), BF16),
-                pltpu.VMEM((NY, LANES), BF16),
-                pltpu.VMEM((ZB, S, 2 * NUMS, XB), BF16),
-                pltpu.VMEM((S, ZB, 3, RY, XB), BF16),
-                pltpu.VMEM((S, ZB, 2 * NUMS, XB), BF16),
-                pltpu.VMEM((S, RY, LANES), BF16),
+                pltpu.VMEM((PY, YB // 2, LANES), BF16),
+                pltpu.VMEM((ZB, 2, S, RY, XB), BF16),
+                pltpu.VMEM((ZB, S, RY + 2 * NUMS, XB), BF16),
+                pltpu.VMEM((NY // 2, LANES), BF16),
+                pltpu.VMEM((S, ZB, 2, RY, XB), BF16),
+                pltpu.VMEM((S, ZB, RY + 2 * NUMS, XB), BF16),
+                pltpu.VMEM((S, RY // 2, LANES), BF16),
                 pltpu.VMEM((K * RY, LANES), F32),
                 pltpu.VMEM((2, K * RY, XB + LANES), BF16),
                 pltpu.VMEM((2, K * RY, XB + LANES), BF16),
@@ -438,13 +457,13 @@
                 pltpu.VMEM((fields, K * RY, XB), BF16),
                 pltpu.VMEM((ZB, PZ, fields, groups, 8, XB), BF16),
                 dma((ZB, 3, PY - 1)), dma((ZB, 3, PY - 1)), dma((PY - 1,)), dma((PY - 1,)),
-                dma((ZB, 3, S - 1)), dma((ZB, 3, S - 1)), dma((ZB, S - 1)), dma((ZB, S - 1)),
+                dma((ZB, 3, S - 1)), dma((ZB, 3, S - 1)),
                 dma((S - 1,)), dma((S - 1,)), dma((ZB, 2, PZ - 1)), dma((ZB, 2, PZ - 1)),
-                dma((8,)), dma((1,)), dma((ZB,)), dma((1,)), dma((ZB,)), dma((ZB,)), dma((1,)), dma((ZB, 2)),
+                dma((8,)), dma((1,)), dma((ZB, 3)), dma((1,)), dma((ZB, 3)), dma((1,)), dma((ZB, 2)),
             ],
             compiler_params=pltpu.CompilerParams(
                 collective_id=0, has_side_effects=True, vmem_limit_bytes=56 * 1024 * 1024),
-        )(velocity, *tables, metric_x[None, :], metric_y, sketch_matrix.T)
+        )(velocity.reshape(1, 3, ZB, YB // RY, RY, NX), *tables, metric_x[None, :], metric_y, sketch_matrix.T)
         per = 8 // K
         whole_block = lambda t: pl.BlockSpec(t.shape, lambda g: (0,) * t.ndim)
         metric_row = metric_z[None, :]

time: 122 us -> 118 us (0.967)
  Pallas kernels: 121 us -> 118 us
    pallas_call x1, Pallas kernels: 115 us -> 112 us  [step(): pl.pallas_call(functools.partial(body, z), out_shape=jax.ShapeDtypeStruct...]
where the time goes in v4:
time: 118 us
  Pallas kernels  118 us (100%)
    pallas_call x1, Pallas kernels, step(): pl.pallas_call(functools.partial(body, z), out_shape=jax.ShapeDtypeStruct...  112 us
    pallas_call x1, Pallas kernels, step(): pl.pallas_call(functools.partial(z_body, z), grid=(groups,), out_shape=ja...  6.55 us

profile of v4, /device:TPU:1, one launch (start us, length us, event | category | flops | bytes accessed | tf_op | source)
XLA Modules:
  0.0 118.1 jit_solution(4940976724593695434)
XLA Ops:
  0.0 111.6 %shard_map.118.lines = bf16[7,3,384,256]{3,2,1,0:T(8,128)(2,1)} custom-call(bf16[1,3,6,2,48,1024]{5,4,3,2,1,0:T(8,128)(2,1)} %bitcast.5, bf16[2,1024,128]{2,1,0:T(8,128)(2,1)} %constant.14.clone.gx_in, bf16[2,2,64,384]{3,2,1,0:T(8,128)(2,1)} %constant.15.clone.gy_in, bf16[2,2,384,256]{3,2,1,0:T(8,128)(2,1)} %constant.16.clone.tx_in, ...), custom_call_target="tpu_custom_call" | custom-call | tf_op jit(solution)/shard_map/pallas_call | solution.py:433
  111.6 6.6 %shard_map.119 = f32[4,3,6,48,256]{4,3,2,1,0:T(8,128)} custom-call(bf16[7,3,384,256]{3,2,1,0:T(8,128)(2,1)} %shard_map.118.lines, bf16[2,384,384]{2,1,0:T(8,128)(2,1)} %constant.19.clone.dz, bf16[384,384]{1,0:T(8,128)(2,1)} %constant.23.turn, f32[1,48]{1,0:T(1,128)} %bitcast.8), custom_call_target="tpu_custom_call" | custom-call | tf_op jit(solution)/shard_map/pallas_call | solution.py:470

commit v5 on v4

--- a/solution.py
+++ b/solution.py
@@ -174,7 +174,7 @@
     def b_rows(p):
         return pl.ds(pl.multiple_of((me_z * ZB + p) * 8, 8), 8)
 
-    part_of = (slice(0, 5), slice(5, 7))
+    part_of = (slice(0, 5), slice(5, 6), slice(6, 7))
 
     def b_copy(p, part, d):
         peer = other(me_z, d, PZ)
@@ -352,12 +352,16 @@
         came(p, 2)
         sketch_field(p, 2)
         sketch_numbers(p, 1)
-        x_slopes, y_slopes = x_slope(1), y_slope(1)
+        x_slopes = x_slope(1)
+        for k in range(K):
+            own = slice(RY * k, RY * (k + 1))
+            pb[5, own, :] = (x_slopes[own] * mx[...]).astype(BF16)
+        send_part(p, 1)
+        y_slopes = y_slope(1)
         for k in range(K):
             own, cols = slice(RY * k, RY * (k + 1)), slice(XB * k, XB * (k + 1))
-            pb[5, own, :] = (x_slopes[own] * mx[...]).astype(BF16)
             pb[6, own, :] = (y_slopes[:, cols] * scale_y[...]).astype(BF16)
-        send_part(p, 1)
+        send_part(p, 2)
 
     @pl.loop(0, ZB + lag + 1)
     def _(i):
@@ -386,7 +390,7 @@
             w_stage(i - lag - 1)
 
     for p in range(ZB):
-        for part in range(2):
+        for part in range(3):
             b_local(p, part).wait()
             for d in far_first(PZ):
                 b_copy(p, part, d).wait_recv()
@@ -397,7 +401,7 @@
                 a_copy(p, f, d).wait_send()
             for d in far_first(S):
                 c_copy(p, f, d).wait_send()
-        for part in range(2):
+        for part in range(3):
             for d in far_first(PZ):
                 b_copy(p, part, d).wait_send()
     for d in far_first(PY):
@@ -458,8 +462,8 @@
                 pltpu.VMEM((ZB, PZ, fields, groups, 8, XB), BF16),
                 dma((ZB, 3, PY - 1)), dma((ZB, 3, PY - 1)), dma((PY - 1,)), dma((PY - 1,)),
                 dma((ZB, 3, S - 1)), dma((ZB, 3, S - 1)),
-                dma((S - 1,)), dma((S - 1,)), dma((ZB, 2, PZ - 1)), dma((ZB, 2, PZ - 1)),
-                dma((8,)), dma((1,)), dma((ZB, 3)), dma((1,)), dma((ZB, 3)), dma((1,)), dma((ZB, 2)),
+                dma((S - 1,)), dma((S - 1,)), dma((ZB, 3, PZ - 1)), dma((ZB, 3, PZ - 1)),
+                dma((8,)), dma((1,)), dma((ZB, 3)), dma((1,)), dma((ZB, 3)), dma((1,)), dma((ZB, 3)),
             ],
             compiler_params=pltpu.CompilerParams(
                 collective_id=0, has_side_effects=True, vmem_limit_bytes=56 * 1024 * 1024),

time: 118 us -> 119 us (level)
  no operation moved by 1% of the time
where the time goes in v5:
time: 119 us
  Pallas kernels  119 us (100%)
    pallas_call x1, Pallas kernels, step(): pl.pallas_call(functools.partial(body, z), out_shape=jax.ShapeDtypeStruct...  112 us
    pallas_call x1, Pallas kernels, step(): pl.pallas_call(functools.partial(z_body, z), grid=(groups,), out_shape=ja...  6.55 us

profile of v5, /device:TPU:1, one launch (start us, length us, event | category | flops | bytes accessed | tf_op | source)
XLA Modules:
  0.0 118.7 jit_solution(15905003718759516064)
XLA Ops:
  0.0 112.2 %shard_map.118.lines = bf16[7,3,384,256]{3,2,1,0:T(8,128)(2,1)} custom-call(bf16[1,3,6,2,48,1024]{5,4,3,2,1,0:T(8,128)(2,1)} %bitcast.5, bf16[2,1024,128]{2,1,0:T(8,128)(2,1)} %constant.14.clone.gx_in, bf16[2,2,64,384]{3,2,1,0:T(8,128)(2,1)} %constant.15.clone.gy_in, bf16[2,2,384,256]{3,2,1,0:T(8,128)(2,1)} %constant.16.clone.tx_in, ...), custom_call_target="tpu_custom_call" | custom-call | tf_op jit(solution)/shard_map/pallas_call | solution.py:437
  112.2 6.6 %shard_map.119 = f32[4,3,6,48,256]{4,3,2,1,0:T(8,128)} custom-call(bf16[7,3,384,256]{3,2,1,0:T(8,128)(2,1)} %shard_map.118.lines, bf16[2,384,384]{2,1,0:T(8,128)(2,1)} %constant.19.clone.dz, bf16[384,384]{1,0:T(8,128)(2,1)} %constant.23.turn, f32[1,48]{1,0:T(1,128)} %bitcast.8), custom_call_target="tpu_custom_call" | custom-call | tf_op jit(solution)/shard_map/pallas_call | solution.py:474
